TPU v7x, 128 devices: a whole 4x4x4 slice. The times are simulated.
128 devices in a mesh: row: 16 (over y_lo, z, core), col: 8 (over x, y_hi).
Axes of the slice: x: 4, y: 4 (y_hi: 2, y_lo: 2; y = y_hi * 2 + y_lo), z: 4, core: 2. Of those that a mesh axis runs over, the one named last changes fastest.
Arguments:
- weather: bfloat16 [192, 1024, 1024], P(None, 'row', 'col'), may hold values from -6 to 6
- cotangent: bfloat16 [192, 1024, 1024], P(None, 'row', 'col'), may hold values from -6 to 6
- spectral_in: bfloat16 [2, 2, 96, 96], replicated, may hold values from -0.4375 to 0.4375
- spectral_bias: float32 [2, 2, 96], replicated, may hold values from -3 to 3
- spectral_out: bfloat16 [2, 2, 96, 96], replicated, may hold values from -1.75 to 1.75
- project_in: bfloat16 [192, 768], replicated, may hold values from -0.4375 to 0.4375
- project_out: bfloat16 [768, 192], replicated, may hold values from -0.21875 to 0.21875
Outputs:
- layer_out: bfloat16 [192, 1024, 1024], P(None, 'row', 'col')
- grad_weather: bfloat16 [192, 1024, 1024], P(None, 'row', 'col')
- grad_project_in: float32 [192, 768], replicated
- grad_project_out: float32 [768, 192], replicated
- grad_spectral_in: float32 [2, 2, 96, 96], replicated
- grad_spectral_out: float32 [2, 2, 96, 96], replicated
- grad_spectral_bias: float32 [2, 2, 96], replicated
All inputs are finite; a program needn't handle non-finite values.
Results may differ from a plain program's by a relative error of at most 0.019.
The roundings to bfloat16 on the way count: a program that leaves them out, or rounds other values in their place, can miss the bound.
Values may be sent and summed in bfloat16 or wider, within the bound.
A program may use at most 192 MiB of HBM per device.

v0:
```python
from functools import partial
import math

import jax
import jax.numpy as jnp
from jax import lax
from jax.sharding import PartitionSpec as P

H = 1024
W = 1024
NB = 2
BS = 96
KH = 512
KW = 256


epsilon = 1e-05
threshold = 0.1


def product(form, left, right):
    return jnp.einsum(form, left, right, preferred_element_type=jnp.float32)


def gelu_slope(values):
    return 0.5 * (1.0 + lax.erf(values * (1.0 / math.sqrt(2.0)))) + values * jnp.exp(
        -0.5 * values * values
    ) * (1.0 / math.sqrt(2.0 * math.pi))


def width_tables(width, kept):
    position = jnp.arange(width, dtype=jnp.int32)
    frequency = jnp.arange(kept, dtype=jnp.int32)
    phases = position[:, None] * frequency[None, :] % width
    angles = phases.astype(jnp.float32) * (2.0 * math.pi / width)
    factor = 1.0 / math.sqrt(width)
    weight = jnp.where(frequency == 0, 1.0, 2.0).astype(jnp.float32)
    cosine = jnp.cos(angles) * factor
    sine_values = -jnp.sin(angles) * factor
    return (
        cosine.astype(jnp.bfloat16),
        sine_values.astype(jnp.bfloat16),
        (cosine * weight[None, :]).astype(jnp.bfloat16),
        (sine_values * weight[None, :]).astype(jnp.bfloat16),
    )


def height_tables(height, kept):
    position = jnp.arange(height, dtype=jnp.int32)
    indices = jnp.arange(kept, dtype=jnp.int32)
    frequency = jnp.where(indices < kept // 2, indices, indices + (height - kept))
    phases = position[:, None] * frequency[None, :] % height
    angles = phases.astype(jnp.float32) * (2.0 * math.pi / height)
    factor = 1.0 / math.sqrt(height)
    return (
        (jnp.cos(angles) * factor).astype(jnp.bfloat16),
        (-jnp.sin(angles) * factor).astype(jnp.bfloat16),
    )


def width_forward(field_part, cosine_table, sine_table):
    real_part = product("crw,wk->rkc", field_part, cosine_table)
    imaginary = product("crw,wk->rkc", field_part, sine_table)
    return jnp.stack([real_part, imaginary], axis=2).astype(jnp.bfloat16)


def width_inverse(spectrum, cosine_table, sine_table):
    half_width = spectrum.shape[2] // 2
    summed = product("rkc,wk->crw", spectrum[:, :, :half_width], cosine_table)
    summed = summed + product("rkc,wk->crw", spectrum[:, :, half_width:], sine_table)
    return summed.astype(jnp.bfloat16)


def height_forward(spectrum, real_table, imaginary_table):
    half_width = spectrum.shape[2] // 2
    first_term = product("hnx,hm->mnx", spectrum, real_table)
    second = product("hnx,hm->mnx", spectrum, imaginary_table)
    return jnp.concatenate(
        [
            first_term[:, :, :half_width] - second[:, :, half_width:],
            first_term[:, :, half_width:] + second[:, :, :half_width],
        ],
        axis=2,
    )


def height_inverse(kept_modes, real_table, imaginary_table):
    half_width = kept_modes.shape[2] // 2
    first_term = product("mnx,hm->hnx", kept_modes, real_table)
    second = product("mnx,hm->hnx", kept_modes, imaginary_table)
    return jnp.concatenate(
        [
            first_term[:, :, :half_width] + second[:, :, half_width:],
            first_term[:, :, half_width:] - second[:, :, :half_width],
        ],
        axis=2,
    )


def soft_shrink(values):
    return values - threshold * jnp.tanh(values * (1.0 / threshold))


def shrink_slope(values):
    return jnp.square(jnp.tanh(values * (1.0 / threshold)))


def spectral_forward(kept_modes, spectral_in, spectral_bias, spectral_out):
    mode_count, column_count, doubled = kept_modes.shape
    pieces = kept_modes.reshape(mode_count, column_count, 2, NB, BS)
    real_input, imaginary_input = (pieces[:, :, 0], pieces[:, :, 1])
    before_real = (
        product("mnbi,bio->mnbo", real_input, spectral_in[0])
        - product("mnbi,bio->mnbo", imaginary_input, spectral_in[1])
        + spectral_bias[0]
    )
    before_imaginary = (
        product("mnbi,bio->mnbo", imaginary_input, spectral_in[0])
        + product("mnbi,bio->mnbo", real_input, spectral_in[1])
        + spectral_bias[1]
    )
    hidden_real = jax.nn.gelu(before_real, approximate=False).astype(jnp.bfloat16)
    hidden_imaginary = jax.nn.gelu(before_imaginary, approximate=False).astype(jnp.bfloat16)
    second_real = product("mnbi,bio->mnbo", hidden_real, spectral_out[0]) - product(
        "mnbi,bio->mnbo", hidden_imaginary, spectral_out[1]
    )
    second_imaginary = product("mnbi,bio->mnbo", hidden_imaginary, spectral_out[0]) + product(
        "mnbi,bio->mnbo", hidden_real, spectral_out[1]
    )
    shrunk = jnp.stack([soft_shrink(second_real), soft_shrink(second_imaginary)], axis=2)
    shrunk = shrunk.reshape(mode_count, column_count, doubled).astype(jnp.bfloat16)
    return (
        shrunk,
        (
            before_real,
            before_imaginary,
            hidden_real,
            hidden_imaginary,
            second_real,
            second_imaginary,
        ),
    )


def spectral_backward(gradient, kept_modes, saved, spectral_in, spectral_out):
    mode_count, column_count, doubled = gradient.shape
    grad_pieces = gradient.reshape(mode_count, column_count, 2, NB, BS)
    pieces = kept_modes.reshape(mode_count, column_count, 2, NB, BS)
    real_input, imaginary_input = (pieces[:, :, 0], pieces[:, :, 1])
    before_real, before_imaginary, hidden_real, hidden_imaginary, second_real, second_imaginary = (
        saved
    )
    keep_real = (grad_pieces[:, :, 0] * shrink_slope(second_real)).astype(jnp.bfloat16)
    keep_imaginary = (grad_pieces[:, :, 1] * shrink_slope(second_imaginary)).astype(jnp.bfloat16)
    back_real = product("mnbo,bio->mnbi", keep_real, spectral_out[0]) + product(
        "mnbo,bio->mnbi", keep_imaginary, spectral_out[1]
    )
    back_imaginary = product("mnbo,bio->mnbi", keep_imaginary, spectral_out[0]) - product(
        "mnbo,bio->mnbi", keep_real, spectral_out[1]
    )
    out_real = product("mnbi,mnbo->bio", hidden_real, keep_real) + product(
        "mnbi,mnbo->bio", hidden_imaginary, keep_imaginary
    )
    out_imaginary = product("mnbi,mnbo->bio", hidden_real, keep_imaginary) - product(
        "mnbi,mnbo->bio", hidden_imaginary, keep_real
    )
    gate_real = (back_real * gelu_slope(before_real)).astype(jnp.bfloat16)
    gate_imaginary = (back_imaginary * gelu_slope(before_imaginary)).astype(jnp.bfloat16)
    in_real = product("mnbi,mnbo->bio", real_input, gate_real) + product(
        "mnbi,mnbo->bio", imaginary_input, gate_imaginary
    )
    in_imaginary = product("mnbi,mnbo->bio", real_input, gate_imaginary) - product(
        "mnbi,mnbo->bio", imaginary_input, gate_real
    )
    bias_grad = jnp.stack(
        [
            jnp.sum(gate_real.astype(jnp.float32), axis=(0, 1)),
            jnp.sum(gate_imaginary.astype(jnp.float32), axis=(0, 1)),
        ]
    )
    input_real = product("mnbo,bio->mnbi", gate_real, spectral_in[0]) + product(
        "mnbo,bio->mnbi", gate_imaginary, spectral_in[1]
    )
    input_imaginary = product("mnbo,bio->mnbi", gate_imaginary, spectral_in[0]) - product(
        "mnbo,bio->mnbi", gate_real, spectral_in[1]
    )
    grad_modes = jnp.stack([input_real, input_imaginary], axis=2)
    grad_modes = grad_modes.reshape(mode_count, column_count, doubled).astype(jnp.bfloat16)
    return (
        grad_modes,
        jnp.stack([in_real, in_imaginary]),
        jnp.stack([out_real, out_imaginary]),
        bias_grad,
    )


def layer_norm(flat_field):
    centred = flat_field - jnp.mean(flat_field, axis=0, keepdims=True)
    variance = jnp.mean(centred * centred, axis=0, keepdims=True)
    inverse_spread = lax.rsqrt(variance + epsilon)
    return (centred * inverse_spread, inverse_spread)


def norm_backward(normed, inverse_spread, gradient):
    mean_grad = jnp.mean(gradient, axis=0, keepdims=True)
    mean_cross = jnp.mean(gradient * normed, axis=0, keepdims=True)
    return inverse_spread * (gradient - mean_grad - normed * mean_cross)


def token_block(weather, normed_in, filtered, cotangent, project_in, project_out):
    channels = weather.shape[0]
    summed = (
        weather.astype(jnp.float32) + normed_in.astype(jnp.float32) + filtered.astype(jnp.float32)
    )
    flat_sum = summed.reshape(channels, -1)
    normed, inverse_spread = layer_norm(flat_sum)
    normed_low = normed.astype(jnp.bfloat16)
    before = product("cn,ch->hn", normed_low, project_in)
    hidden = jax.nn.gelu(before, approximate=False).astype(jnp.bfloat16)
    output = (flat_sum + product("hn,hc->cn", hidden, project_out)).astype(jnp.bfloat16)
    flat_cot = cotangent.reshape(channels, -1)
    back_hidden = product("cn,hc->hn", flat_cot, project_out)
    back_before = (back_hidden * gelu_slope(before)).astype(jnp.bfloat16)
    grad_out = product("hn,cn->hc", hidden, flat_cot)
    grad_in = product("cn,hn->ch", normed_low, back_before)
    back_normed = product("hn,ch->cn", back_before, project_in)
    grad_sum = flat_cot.astype(jnp.float32) + norm_backward(normed, inverse_spread, back_normed)
    return (output.reshape(weather.shape), grad_sum.reshape(weather.shape), grad_in, grad_out)


def to_columns(field_part, transform):
    channels = field_part.shape[0]
    shaped = transform(lax.all_to_all(field_part, "col", split_axis=1, concat_axis=2, tiled=True))
    return shaped.reshape(shaped.shape[0], shaped.shape[1], 2 * channels)


def from_columns(field_part):
    return lax.all_to_all(field_part, "col", split_axis=2, concat_axis=1, tiled=True)


def to_modes(spectrum):
    return lax.all_to_all(spectrum, ("row", "col"), split_axis=1, concat_axis=0, tiled=True)


def to_rows(spectrum):
    return lax.all_to_all(spectrum, ("row", "col"), split_axis=0, concat_axis=1, tiled=True)


def body(weather, cotangent, spectral_in, spectral_bias, spectral_out, project_in, project_out):
    cosine, sine_table, cosine_weighted, sine_weighted = width_tables(W, KW)
    real_table, imaginary_table = height_tables(H, KH)
    channels = weather.shape[0]
    field_now, cot_now = (weather, cotangent)
    normed_first, spread_first = layer_norm(field_now.astype(jnp.float32).reshape(channels, -1))
    normed_in = normed_first.astype(jnp.bfloat16).reshape(field_now.shape)
    spectrum = to_columns(
        normed_in, partial(width_forward, cosine_table=cosine, sine_table=sine_table)
    )
    kept_low = height_forward(to_modes(spectrum), real_table, imaginary_table).astype(jnp.bfloat16)
    shrunk, saved = spectral_forward(kept_low, spectral_in, spectral_bias, spectral_out)
    back = to_rows(height_inverse(shrunk, real_table, imaginary_table).astype(jnp.bfloat16))
    filtered = from_columns(width_inverse(back, cosine_weighted, sine_weighted))
    output, grad_sum, grad_in, grad_out = token_block(
        field_now, normed_in, filtered, cot_now, project_in, project_out
    )
    grad_spectrum = to_columns(
        grad_sum.astype(jnp.bfloat16),
        partial(width_forward, cosine_table=cosine_weighted, sine_table=sine_weighted),
    )
    grad_kept = height_forward(to_modes(grad_spectrum), real_table, imaginary_table)
    grad_modes, grad_first, grad_second, grad_bias = spectral_backward(
        grad_kept, kept_low, saved, spectral_in, spectral_out
    )
    grad_back = to_rows(
        height_inverse(grad_modes, real_table, imaginary_table).astype(jnp.bfloat16)
    )
    grad_filtered = from_columns(width_inverse(grad_back, cosine, sine_table))
    grad_normed = grad_sum + grad_filtered.astype(jnp.float32)
    grad_flat = grad_sum.reshape(channels, -1) + norm_backward(
        normed_first, spread_first, grad_normed.reshape(channels, -1)
    )
    grad_weather = grad_flat.reshape(field_now.shape).astype(jnp.bfloat16)
    grad_in, grad_out, grad_first, grad_second, grad_bias = lax.psum(
        (grad_in, grad_out, grad_first, grad_second, grad_bias), ("row", "col")
    )
    return (
        output,
        grad_weather,
        grad_in / H,
        grad_out / H,
        grad_first / H,
        grad_second / H,
        grad_bias / H,
    )


def solution(mesh):
    in_specs = (P(None, "row", "col"), P(None, "row", "col"), P(), P(), P(), P(), P())
    out_specs = (P(None, "row", "col"), P(None, "row", "col"), P(), P(), P(), P(), P())
    return jax.shard_map(body, mesh=mesh, in_specs=in_specs, out_specs=out_specs, check_vma=False)
```

profile of v0, /device:TPU:1, one launch (start us, length us, event | category | flops | bytes accessed | tf_op | source)
XLA Modules:
  0.0 833.4 jit_solution(13279847729300512138)
XLA Ops:
  7.2 3.9 convert_reduce_fusion
  17.2 45.8 %all_to_all.126 = bf16[192,64,128]{2,0,1:T(8,128)(2,1)S(1)} all-to-all(bf16[192,64,128]{2,0,1:T(8,128)(2,1)S(1)} %fusion.28), channel_id=1, replica_groups=mesh['row'=16,'col'=8] {'col'}, dimensions={1} | all-to-all | bytes 6291456 | tf_op jit(solution)/shard_map/all_to_all | solution.py:233
  63.1 3.8 copy.301
  66.9 5.8 all_to_all.95
  72.6 6.6 fusion.69
  79.2 5.3 fusion.68
  88.9 9.4 %all-to-all-start.1 = ((bf16[8,256,384]{2,0,1:T(8,128)(2,1)}), bf16[8,256,384]{2,0,1:T(8,128)(2,1)}, u32[]{:S(2)}, u32[]{:S(2)}) async-start(bf16[8,256,384]{2,0,1:T(8,128)(2,1)} %copy.91), calls=%async_computation.1 | async-start | bytes 3145728 | tf_op jit(solution)/shard_map/all_to_all | solution.py:242
  98.3 22.3 %all-to-all-done.1 = bf16[8,256,384]{2,0,1:T(8,128)(2,1)} async-done(((bf16[8,256,384]{2,0,1:T(8,128)(2,1)}), bf16[8,256,384]{2,0,1:T(8,128)(2,1)}, u32[]{:S(2)}, u32[]{:S(2)}) %all-to-all-start.1) | async-done | bytes 1572896 | tf_op jit(solution)/shard_map/all_to_all | solution.py:242
  120.7 9.7 %fusion.60 = f32[512,2,384]{0,2,1:T(8,128)S(1)} fusion(bf16[128,8,2,384]{3,1,2,0:T(8,128)(2,1)} %bitcast.11, s32[512]{0:T(512)S(1)} %compare_select_fusion), kind=kOutput, calls=%fused_computation.104 | convolution fusion | flops 814219264 | bytes 3147776 | tf_op jit(solution)/shard_map/hnx,hm->mnx/dot_general | solution.py:22
  130.3 9.8 %fusion.62 = f32[512,2,384]{0,2,1:T(8,128)S(1)} fusion(bf16[128,8,2,384]{3,1,2,0:T(8,128)(2,1)} %bitcast.11, s32[512]{0:T(512)S(1)} %compare_select_fusion), kind=kOutput, calls=%fused_computation.106 | convolution fusion | flops 813694976 | bytes 3147776 | tf_op jit(solution)/shard_map/hnx,hm->mnx/dot_general | solution.py:22
  149.3 8.9 %fusion.104 = f32[1024,2,384]{0,2,1:T(8,128)S(1)} fusion(bf16[512,2,384]{0,2,1:T(8,128)(2,1)S(1)} %bitcast.548, s32[512]{0:T(512)S(1)} %compare_select_fusion), kind=kOutput, calls=%fused_computation.179 | convolution fusion | flops 814219264 | bytes 3934208 | tf_op jit(solution)/shard_map/mnx,hm->hnx/dot_general | solution.py:22
  158.2 8.5 %fusion.110 = f32[1024,2,384]{0,2,1:T(8,128)S(1)} fusion(bf16[512,2,384]{0,2,1:T(8,128)(2,1)S(1)} %bitcast.549, s32[512]{0:T(512)S(1)} %compare_select_fusion), kind=kOutput, calls=%fused_computation.181 | convolution fusion | flops 813694976 | bytes 3934208 | tf_op jit(solution)/shard_map/mnx,hm->hnx/dot_general | solution.py:22
  168.8 4.9 copy.104
  173.8 6.5 all-to-all-start.2
  180.3 22.7 %all-to-all-done.2 = bf16[1024,2,384]{2,1,0:T(2,128)(2,1)} async-done(((bf16[1024,2,384]{2,1,0:T(2,128)(2,1)}), bf16[1024,2,384]{2,1,0:T(2,128)(2,1)}, u32[]{:S(2)}, u32[]{:S(2)}) %all-to-all-start.2) | async-done | bytes 1572896 | tf_op jit(solution)/shard_map/all_to_all | solution.py:246
  211.8 5.8 fusion.157
  217.6 4.6 fusion.158
  225.0 7.3 copy.109
  232.3 53.7 %all_to_all.127 = bf16[192,8,1024]{0,1,2:T(8,128)(2,1)} all-to-all(bf16[192,8,1024]{0,1,2:T(8,128)(2,1)} %copy.109), channel_id=1, replica_groups=mesh['row'=16,'col'=8] {'col'}, dimensions={2} | all-to-all | bytes 6291456 | tf_op jit(solution)/shard_map/all_to_all | solution.py:238
  286.0 7.5 copy.110
  293.5 5.7 fusion.295
  300.5 61.2 %fusion.2 = (bf16[768,8192]{0,1:T(8,128)(2,1)}, f32[8192,768]{1,0:T(8,128)}) fusion(bf16[192,768]{1,0:T(8,128)(2,1)S(1)} %copy-done, f32[8192]{0:T(1024)S(1)} %rsqrt_bitcast_fusion, f32[8192]{0:T(1024)S(1)} %get-tuple-element.35, f32[192,64,128]{2,0,1:T(8,128)S(1)} %get-tuple-element.16), kind=kOutput, calls=%fused_computation.4 | convolution fusion | flops 2829582336 | bytes 44400640 | tf_op jit(solution)/shard_map/cn,ch->hn/dot_general | solution.py:22
  361.7 19.6 %fusion.8 = bf16[768,8192]{0,1:T(8,128)(2,1)S(1)} fusion(f32[8192,768]{1,0:T(8,128)} %get-tuple-element.44, bf16[768,192]{0,1:T(8,128)(2,1)S(1)} %copy-done.31, bf16[24,8,64,128]{3,2,1,0:T(8,128)(2,1)S(1)} %bitcast.532), kind=kOutput, calls=%fused_computation.10 | convolution fusion | flops 2478833664 | bytes 41189376 | tf_op jit(solution)/shard_map/cn,hc->hn/dot_general | solution.py:22
  381.3 6.5 fusion.35
  392.3 11.9 %convert_bitcast_fusion.1 = (bf16[24,64,8,128]{3,2,1,0:T(8,128)(2,1)S(1)}, f32[192,8192]{1,0:T(8,128)}) fusion(f32[8192]{0:T(1024)S(1)} %broadcast_multiply_fusion.6, f32[8192]{0:T(1024)S(1)} %get-tuple-element.35, f32[8192]{0:T(1024)S(1)} %broadcast_multiply_fusion.7, f32[8192,192]{0,1:T(8,128)} %get-tuple-element.46, f32[8192]{0:T(1024)S(1)} %rsqrt_bitcast_fusion, ...), kind=kLoop, calls=%fused_computation.72 | loop fusion | flops 14155776 | bytes 25296896
  405.0 39.4 %all_to_all.128 = bf16[192,64,128]{2,0,1:T(8,128)(2,1)S(1)} all-to-all(bf16[192,64,128]{2,0,1:T(8,128)(2,1)S(1)} %bitcast.517), channel_id=1, replica_groups=mesh['row'=16,'col'=8] {'col'}, dimensions={1} | all-to-all | bytes 6291456 | tf_op jit(solution)/shard_map/all_to_all | solution.py:233
  449.8 6.6 fusion.71
  456.4 5.3 fusion.70
  464.1 10.6 %all-to-all-start.5 = ((bf16[8,256,384]{2,0,1:T(8,128)(2,1)}), bf16[8,256,384]{2,0,1:T(8,128)(2,1)S(1)}, u32[]{:S(2)}, u32[]{:S(2)}) async-start(bf16[8,256,384]{2,0,1:T(8,128)(2,1)} %copy.116), calls=%async_computation.5 | async-start | bytes 3145728 | tf_op jit(solution)/shard_map/all_to_all | solution.py:242
  474.7 9.8 %fusion.159 = f32[192,768]{1,0:T(8,128)} fusion(bf16[768,8192]{0,1:T(8,128)(2,1)} %copy-done.39, f32[8192]{0:T(1024)S(1)} %rsqrt_bitcast_fusion, f32[8192]{0:T(1024)S(1)} %get-tuple-element.35, f32[192,64,128]{2,0,1:T(8,128)} %copy-done.3), kind=kOutput, calls=%fused_computation.259 | convolution fusion | flops 2420637696 | bytes 19529728 | tf_op jit(solution)/shard_map/cn,hn->ch/dot_general | solution.py:22
  484.5 12.8 %all-to-all-done.5 = bf16[8,256,384]{2,0,1:T(8,128)(2,1)S(1)} async-done(((bf16[8,256,384]{2,0,1:T(8,128)(2,1)}), bf16[8,256,384]{2,0,1:T(8,128)(2,1)S(1)}, u32[]{:S(2)}, u32[]{:S(2)}) %all-to-all-start.5) | async-done | bytes 1572896 | tf_op jit(solution)/shard_map/all_to_all | solution.py:242
  497.3 8.2 fusion.56
  505.5 8.6 %fusion.58 = f32[512,2,384]{0,2,1:T(8,128)S(1)} fusion(bf16[128,8,2,384]{3,1,2,0:T(8,128)(2,1)S(1)} %bitcast.541, s32[512]{0:T(512)S(1)} %copy-done.38), kind=kOutput, calls=%fused_computation.102 | convolution fusion | flops 813694976 | bytes 3147776 | tf_op jit(solution)/shard_map/hnx,hm->mnx/dot_general | solution.py:22
  519.1 8.6 %fusion.101 = f32[1024,2,384]{0,2,1:T(8,128)S(1)} fusion(bf16[512,2,384]{0,2,1:T(8,128)(2,1)S(1)} %bitcast.546, s32[512]{0:T(512)S(1)} %copy-done.38), kind=kOutput, calls=%fused_computation.178 | convolution fusion | flops 814219264 | bytes 3934208 | tf_op jit(solution)/shard_map/mnx,hm->hnx/dot_general | solution.py:22
  527.7 8.7 %fusion.107 = f32[1024,2,384]{0,2,1:T(8,128)S(1)} fusion(bf16[512,2,384]{0,2,1:T(8,128)(2,1)S(1)} %bitcast.547, s32[512]{0:T(512)S(1)} %copy-done.38), kind=kOutput, calls=%fused_computation.180 | convolution fusion | flops 813694976 | bytes 3934208 | tf_op jit(solution)/shard_map/mnx,hm->hnx/dot_general | solution.py:22
  540.3 5.8 all-to-all-start.6
  546.1 10.2 %fusion.40 = f32[768,192]{0,1:T(8,128)} fusion(bf16[768,8192]{0,1:T(8,128)(2,1)} %get-tuple-element.43, bf16[24,8,64,128]{3,2,1,0:T(8,128)(2,1)} %bitcast.531), kind=kOutput, calls=%fused_computation.66 | convolution fusion | flops 2415919104 | bytes 16318464 | tf_op jit(solution)/shard_map/hn,cn->hc/dot_general | solution.py:22
  560.1 8.8 %all-to-all-done.6 = bf16[1024,2,384]{2,1,0:T(2,128)(2,1)S(1)} async-done(((bf16[1024,2,384]{2,1,0:T(2,128)(2,1)}), bf16[1024,2,384]{2,1,0:T(2,128)(2,1)S(1)}, u32[]{:S(2)}, u32[]{:S(2)}) %all-to-all-start.6) | async-done | bytes 1572896 | tf_op jit(solution)/shard_map/all_to_all | solution.py:246
  571.8 5.5 fusion.155
  577.3 5.5 fusion.156
  584.7 5.2 copy.136
  589.9 4.9 all-to-all-start.7
  596.7 10.6 %fusion.51 = bf16[24,8,64,128]{3,1,2,0:T(8,128)(2,1)S(1)} fusion(bf16[768,8192]{0,1:T(8,128)(2,1)} %get-tuple-element.43, bf16[768,192]{0,1:T(8,128)(2,1)S(1)} %copy-done.32, f32[192,64,128]{2,0,1:T(8,128)} %copy-done.3), kind=kOutput, calls=%fused_computation.86 | convolution fusion | flops 2419064832 | bytes 22315008 | tf_op jit(solution)/shard_map/hn,hc->cn/dot_general | solution.py:22
  609.9 101.8 %psum.39 = f32[2,2,96]{2,1,0:T(2,128)S(1)} all-reduce(f32[2,2,96]{2,1,0:T(2,128)S(1)} %pad_maximum_fusion.9), channel_id=1, replica_groups=mesh['row'=16,'col'=8] {'row','col'}, use_global_device_ids=true, to_apply=%region_14.15 | all-reduce | flops 384 | bytes 3072 | tf_op jit(solution)/shard_map/psum | solution.py:283
  712.3 69.6 %all-reduce.3.cloned.1.call-done = (f32[192,768]{1,0:T(8,128)}, f32[768,192]{0,1:T(8,128)}, f32[2,2,96,96]{3,2,1,0:T(8,128)}, f32[2,2,96,96]{3,2,1,0:T(8,128)}) async-done(((f32[192,768]{1,0:T(8,128)}, f32[768,192]{0,1:T(8,128)}, f32[2,2,96,96]{3,2,1,0:T(8,128)}, f32[2,2,96,96]{3,2,1,0:T(8,128)}), (f32[192,768]{1,0:T(8,128)}, f32[768,192]{0,1:T(8,128)}, f32[2,2,96,96]{3,2,1,0:T(8,128)}, ...) | async-done | bytes 1474576 | tf_op jit(solution)/shard_map/psum | solution.py:283
  789.0 7.5 copy.137
  796.6 11.6 %fusion.293 = (f32[8192]{0:T(1024)S(1)}, f32[8192]{0:T(1024)S(1)}) fusion(f32[192,8192]{1,0:T(8,128)} %get-tuple-element.14, f32[24,8,64,128]{3,2,1,0:T(8,128)} %bitcast.506, f32[8192]{0:T(1024)S(1)} %copy-done.30, f32[8192]{0:T(1024)S(1)} %copy-done.29, bf16[192,64,128]{2,1,0:T(8,128)(2,1)S(1)} %copy-done.2), kind=kLoop, calls=%fused_computation.411 | loop fusion | flops 10993664 | bytes 15859712 | tf_op jit(solution)/shard_map/reduce_sum | solution.py:205
  808.2 15.5 %fusion.39 = bf16[24,8,64,128]{3,1,2,0:T(8,128)(2,1)S(1)} fusion(f32[192,8192]{1,0:T(8,128)} %get-tuple-element.14, f32[8192]{0:T(1024)S(1)} %broadcast_multiply_fusion.4, f32[8192]{0:T(1024)S(1)} %copy-done.29, f32[8192]{0:T(1024)S(1)} %broadcast_multiply_fusion.5, f32[8192]{0:T(1024)S(1)} %copy-done.30, f32[24,8,64,128]{3,2,1,0:T(8,128)S(1)} %bitcast.509, ...), kind=kLoop, calls=%fused_computation.65 | loop fusion | flops 15728640 | bytes 19005440
  (178 shorter events, 79.4 us)
Async XLA Ops:
  7.2 293.3 %copy-start = (bf16[192,768]{1,0:T(8,128)(2,1)S(1)}, bf16[192,768]{1,0:T(8,128)(2,1)}, u32[]{:S(2)}) copy-start(bf16[192,768]{1,0:T(8,128)(2,1)} %param.12) | copy-start | bytes 884740
  7.2 4.6 copy-start.1
  72.6 6.6 copy-start.19
  85.9 12.3 %copy-start.36 = (f32[2,2,96]{2,1,0:T(2,128)S(1)}, f32[2,2,96]{2,1,0:T(2,128)}, u32[]{:S(2)}) copy-start(f32[2,2,96]{2,1,0:T(2,128)} %param.10) | copy-start | bytes 4612
  88.9 31.8 %all-to-all-start.1 = ((bf16[8,256,384]{2,0,1:T(8,128)(2,1)}), bf16[8,256,384]{2,0,1:T(8,128)(2,1)}, u32[]{:S(2)}, u32[]{:S(2)}) async-start(bf16[8,256,384]{2,0,1:T(8,128)(2,1)} %copy.91), calls=%async_computation.1 | async-start | bytes 3145728 | tf_op jit(solution)/shard_map/all_to_all | solution.py:242
  98.3 59.9 %copy-start.37 = (s32[512]{0:T(512)}, s32[512]{0:T(512)S(1)}, u32[]{:S(2)}) copy-start(s32[512]{0:T(512)S(1)} %compare_select_fusion) | copy-start | bytes 6148
  140.1 0.9 copy-start.23
  140.6 3.8 copy-start.12
  140.6 4.1 copy-start.21
  141.6 2.8 copy-start.25
  144.4 4.1 copy-start.8
  148.8 9.4 %copy-start.4 = (f32[512,2,2,96]{0,3,1,2:T(8,128)}, f32[512,2,2,96]{0,3,1,2:T(8,128)S(1)}, u32[]{:S(2)}) copy-start(f32[512,2,2,96]{0,3,1,2:T(8,128)S(1)} %fusion.77) | copy-start | bytes 2359300
  173.8 29.2 %all-to-all-start.2 = ((bf16[1024,2,384]{2,1,0:T(2,128)(2,1)}), bf16[1024,2,384]{2,1,0:T(2,128)(2,1)}, u32[]{:S(2)}, u32[]{:S(2)}) async-start(bf16[1024,2,384]{2,1,0:T(2,128)(2,1)} %copy.104), calls=%async_computation.2 | async-start | bytes 3145728 | tf_op jit(solution)/shard_map/all_to_all | solution.py:246
  180.3 37.2 %copy-start.34 = (f32[256]{0:T(256)}, f32[256]{0:T(256)S(1)}, u32[]{:S(2)}) copy-start(f32[256]{0:T(256)S(1)} %fusion.213) | copy-start | bytes 3076
  211.8 5.8 copy-start.20
  299.2 82.1 %copy-start.3 = (f32[192,64,128]{2,0,1:T(8,128)}, f32[192,64,128]{2,0,1:T(8,128)S(1)}, u32[]{:S(2)}) copy-start(f32[192,64,128]{2,0,1:T(8,128)S(1)} %get-tuple-element.16) | copy-start | bytes 18874372
  300.5 61.2 %copy-start.17 = (bf16[192,64,128]{2,1,0:T(8,128)(2,1)S(1)}, bf16[192,64,128]{2,1,0:T(8,128)(2,1)}, u32[]{:S(2)}) copy-start(bf16[192,64,128]{2,1,0:T(8,128)(2,1)} %param.8) | copy-start | bytes 9437188
  300.5 61.2 %copy-start.31 = (bf16[768,192]{0,1:T(8,128)(2,1)S(1)}, bf16[768,192]{0,1:T(8,128)(2,1)}, u32[]{:S(2)}) copy-start(bf16[768,192]{0,1:T(8,128)(2,1)} %param.13) | copy-start | bytes 884740
  381.3 6.5 copy-start.39
  446.4 3.3 copy-start.35
  449.8 6.6 copy-start.18
  464.1 33.2 %all-to-all-start.5 = ((bf16[8,256,384]{2,0,1:T(8,128)(2,1)}), bf16[8,256,384]{2,0,1:T(8,128)(2,1)S(1)}, u32[]{:S(2)}, u32[]{:S(2)}) async-start(bf16[8,256,384]{2,0,1:T(8,128)(2,1)} %copy.116), calls=%async_computation.5 | async-start | bytes 3145728 | tf_op jit(solution)/shard_map/all_to_all | solution.py:242
  474.7 22.6 %copy-start.38 = (s32[512]{0:T(512)S(1)}, s32[512]{0:T(512)}, u32[]{:S(2)}) copy-start(s32[512]{0:T(512)} %copy-done.37) | copy-start | bytes 6148
  514.5 1.1 copy-start.7
  514.6 1.3 copy-start.5
  514.6 1.4 copy-start.26
  515.6 1.2 copy-start.40
  515.9 1.5 copy-start.24
  516.1 1.6 copy-start.41
  517.4 41.5 %copy-start.15 = (bf16[512,2,2,96]{0,3,1,2:T(8,128)(2,1)}, bf16[512,2,2,96]{0,3,1,2:T(8,128)(2,1)S(1)}, u32[]{:S(2)}) copy-start(bf16[512,2,2,96]{0,3,1,2:T(8,128)(2,1)S(1)} %get-tuple-element.48) | copy-start | bytes 1179652
  540.3 28.6 %all-to-all-start.6 = ((bf16[1024,2,384]{2,1,0:T(2,128)(2,1)}), bf16[1024,2,384]{2,1,0:T(2,128)(2,1)S(1)}, u32[]{:S(2)}, u32[]{:S(2)}) async-start(bf16[1024,2,384]{2,1,0:T(2,128)(2,1)} %copy.131), calls=%async_computation.6 | async-start | bytes 3145728 | tf_op jit(solution)/shard_map/all_to_all | solution.py:246
  546.1 10.2 %copy-start.9 = (bf16[512,2,2,96]{0,3,1,2:T(8,128)(2,1)S(1)}, bf16[512,2,2,96]{0,3,1,2:T(8,128)(2,1)}, u32[]{:S(2)}) copy-start(bf16[512,2,2,96]{0,3,1,2:T(8,128)(2,1)} %copy-done.8) | copy-start | bytes 1179652
  546.1 10.7 %copy-start.11 = (bf16[512,2,2,96]{0,3,1,2:T(8,128)(2,1)S(1)}, bf16[512,2,2,96]{0,3,1,2:T(8,128)(2,1)}, u32[]{:S(2)}) copy-start(bf16[512,2,2,96]{0,3,1,2:T(8,128)(2,1)} %copy-done.10) | copy-start | bytes 1179652
  556.3 1.7 copy-start.22
  556.3 2.9 copy-start.13
  589.9 5.1 copy-start.27
  589.9 5.8 copy-start.14
  589.9 5.8 copy-start.16
  589.9 5.8 copy-start.33
  589.9 6.1 copy-start.28
  589.9 199.1 %all-to-all-start.7 = ((bf16[192,8,1024]{0,1,2:T(8,128)(2,1)}), bf16[192,8,1024]{0,1,2:T(8,128)(2,1)}, u32[]{:S(2)}, u32[]{:S(2)}) async-start(bf16[192,8,1024]{0,1,2:T(8,128)(2,1)} %copy.136), calls=%async_computation.7 | async-start | bytes 8388608 | tf_op jit(solution)/shard_map/all_to_all | solution.py:238
  594.8 1.9 copy-start.32
  594.8 187.1 %all-reduce.3.cloned.1.call-start = ((), (), s32[]{:S(2)}) async-start(), calls=%async_computation.8 | async-start | bytes 3145728 | tf_op jit(solution)/shard_map/psum | solution.py:283
  789.0 7.5 copy-start.2
  789.0 7.5 copy-start.29
  789.0 7.5 copy-start.30
  796.5 11.7 %slice-start = ((s8[6291456]{0:T(1024)(128)(4,1)}), s8[4194304]{0:T(1024)(128)(4,1)S(1)}, s32[]{:S(2)}) async-start(s8[6291456]{0:T(1024)(128)(4,1)} %bitcast.507), calls=%async_computation.9 | async-start | bytes 8388608
  796.5 11.7 %slice-start.1 = ((s8[6291456]{0:T(1024)(128)(4,1)}), s8[2097152]{0:T(1024)(128)(4,1)S(1)}, s32[]{:S(2)}) async-start(s8[6291456]{0:T(1024)(128)(4,1)} %bitcast.507), calls=%async_computation.10 | async-start | bytes 4194304
  (2 other events, 1.6 us)
Sparse Core Ops, SparseCore 0:
  601.4 180.5 all-reduce.2
where the time goes:
time: 841 us; the launch traced here: 833 us
  matrix products  248 us (29%)
  blocking collectives  241 us (29%)
  waiting for transfers between devices  136 us (16%)
  other arithmetic  79.1 us (9%)
  local copies, waits for them, and re-layouts  76.8 us (9%)
  starting transfers between devices  37.4 us (4%)
  between operations  15.2 us (2%)
    dot_general x42, matrix products, product(): return jnp.einsum(form, left, right, preferred_element_type=jnp.float32)  226 us
    psum x1, blocking collectives, body(): lax.psum((grad_in, grad_out, grad_first, grad_second, grad_bias), ('row',...  102 us
    all_to_all x2, blocking collectives, to_columns(): lax.all_to_all(field_part, 'col', split_axis=1, concat_axis=2, tiled=True)  85.2 us
    psum x1, waiting for transfers between devices, body(): lax.psum((grad_in, grad_out, grad_first, grad_second, grad_bias), ('row',...  69.6 us
    all_to_all x1, blocking collectives, from_columns(): lax.all_to_all(field_part, 'col', split_axis=2, concat_axis=1, tiled=True)  53.7 us
    all_to_all x2, waiting for transfers between devices, to_modes(): lax.all_to_all(spectrum, ('row', 'col'), split_axis=1, concat_axis=0, til...  35.1 us
    all_to_all x2, waiting for transfers between devices, to_rows(): lax.all_to_all(spectrum, ('row', 'col'), split_axis=0, concat_axis=1, til...  31.5 us
    unnamed x3, other arithmetic  27.4 us
  transfers between devices with their start and end apart: 6, of which 5 were waited for; matrix products, arithmetic and copies ran while one was open for 6% of the time, Pallas kernels for 0%

commit v1 on v0

v1 whole, which is shorter than its diff:
```python
from functools import partial
import math

import numpy as np
import jax
import jax.numpy as jnp
from jax import lax
from jax.experimental import pallas as pl
from jax.experimental.pallas import tpu as pltpu
from jax.sharding import PartitionSpec as P

H = 1024
W = 1024
NB = 2
BS = 96
C = 192
HID = 768
KH = 512
KW = 256

LR = 64
LW = 128
CG = 12
CH = 4
NCH = CG // CH
NX = 4
SG = 8
MODES = 2048
EPS = 1e-05
THRESHOLD = 0.1
F32 = jnp.float32
BF16 = jnp.bfloat16
MESH = pl.DeviceIdType.MESH


def tables():
    k = np.arange(KW)
    angle = (k[:, None] * np.arange(W)[None, :] % W).astype(np.float32) * np.float32(2.0 * math.pi / W)
    factor = np.float32(1.0 / math.sqrt(W))
    cosine, sine = np.cos(angle) * factor, -np.sin(angle) * factor
    width = np.stack([cosine.reshape(SG, 32, W), sine.reshape(SG, 32, W)], axis=1).reshape(2 * KW, W)
    weight = np.where(k == 0, 1.0, 2.0).astype(np.float32)[:, None]
    weighted = np.stack(
        [(cosine * weight).reshape(SG, 32, W), (sine * weight).reshape(SG, 32, W)], axis=1
    ).reshape(2 * KW, W)
    m = np.arange(KH)
    frequency = np.where(m < KH // 2, m, m + (H - KH))
    angle = (np.arange(H)[:, None] * frequency[None, :] % H).astype(np.float32) * np.float32(
        2.0 * math.pi / H
    )
    factor = np.float32(1.0 / math.sqrt(H))
    height = np.concatenate([np.cos(angle) * factor, -np.sin(angle) * factor], axis=1)
    return tuple(jnp.asarray(t, F32).astype(BF16) for t in (width, weighted, height))


def dot_nn(left, right):
    return lax.dot_general(left, right, (((1,), (0,)), ((), ())), preferred_element_type=F32)


def dot_nt(left, right):
    return lax.dot_general(left, right, (((1,), (1,)), ((), ())), preferred_element_type=F32)


def dot_tn(left, right):
    return lax.dot_general(left, right, (((0,), (0,)), ((), ())), preferred_element_type=F32)


def normal_parts(values):
    cumulative = 0.5 * (1.0 + lax.erf(values * (1.0 / math.sqrt(2.0))))
    density = jnp.exp(-0.5 * values * values) * (1.0 / math.sqrt(2.0 * math.pi))
    return cumulative, density


class Exchange:
    def __init__(self, scratch):
        (self.X, self.O, self.G, self.K, self.Y0, self.y32, self.Z0, self.Q, self.BK, self.F, self.FO) = scratch[:11]
        self.sems = scratch[11:23]
        self.ri = lax.axis_index("row")
        self.ci = lax.axis_index("col")
        self.core = self.ri % 2
        self.s = self.ri // 2
        self.x = self.ci // 2
        self.yh = self.ci % 2
        self.id1 = self.ci * 2 + self.core
        self.id2 = self.x * 2 + self.core

    def peer1(self, d):
        other = (self.id1 + d) % 16
        return other // 2, other % 2

    def peer2(self, e):
        other = (self.id2 + e) % 8
        return other // 2, other % 2

    def barrier(self):
        sem = pltpu.get_barrier_semaphore()
        for d in range(1, 16):
            col, core = self.peer1(d)
            pl.semaphore_signal(sem, inc=1, device_id=(2 * self.s + core, col), device_id_type=MESH)
        for e in range(1, SG):
            s = (self.s + e) % SG
            pl.semaphore_signal(sem, inc=1, device_id=(2 * s + self.core, self.ci), device_id_type=MESH)
        pl.semaphore_wait(sem, 15 + SG - 1)

    def first_channel(self, col, core):
        return (col % 2) * BS + (col // 2) * (2 * CG) + core * CG

    def copy1(self, src, i, d):
        col, core = self.peer1(d)
        start = self.first_channel(col, core) + i * CH
        rows = pl.ds(pl.multiple_of(self.core * LR, LR), LR)
        return pltpu.make_async_remote_copy(
            src_ref=src.at[pl.ds(start, CH)],
            dst_ref=self.X.at[self.ci, pl.ds(i * CH, CH), rows, :],
            send_sem=self.sems[0].at[i, d],
            recv_sem=self.sems[1].at[i, d],
            device_id=(2 * self.s + core, col),
            device_id_type=MESH,
        )

    def send1(self, src):
        rows = pl.ds(pl.multiple_of(self.core * LR, LR), LR)
        own = self.first_channel(self.ci, self.core)
        for i in range(NCH):
            for d in range(1, 16):
                self.copy1(src, i, d).start()
        self.X[self.ci, :, rows, :] = src[pl.ds(own, CG)]

    def copyb(self, i, e):
        s = (self.s + e) % SG
        return pltpu.make_async_remote_copy(
            src_ref=self.O.at[s, pl.ds(i * CH, CH)],
            dst_ref=self.G.at[self.s, pl.ds(i * CH, CH)],
            send_sem=self.sems[2].at[i, e],
            recv_sem=self.sems[3].at[i, e],
            device_id=(2 * s + self.core, self.ci),
            device_id_type=MESH,
        )

    def width_forward(self, src, table):
        @pl.loop(0, NCH)
        def _(i):
            for d in range(1, 16):
                self.copy1(src, i, d).wait_recv()
            for half in range(CH // 2):
                c = i * CH + 2 * half
                field = jnp.concatenate(
                    [self.X[p, pl.ds(c, 2)].reshape(2 * 2 * LR, LW) for p in range(8)], axis=1
                )
                spectrum = dot_nt(table[...], field).astype(BF16)
                for j in range(2):
                    self.O[:, c + j] = spectrum[:, j * 128 : (j + 1) * 128].reshape(SG, 64, 128)
            for e in range(1, SG):
                self.copyb(i, e).start()
            own = pl.ds(i * CH, CH)
            self.G[self.s, own] = self.O[self.s, own]

    def copyc(self, i, e):
        x, core = self.peer2(e)
        return pltpu.make_async_remote_copy(
            src_ref=self.K.at[x, core, pl.ds(i * CH, CH)],
            dst_ref=self.Y0.at[self.id2, pl.ds(i * CH, CH)],
            send_sem=self.sems[4].at[i, e],
            recv_sem=self.sems[5].at[i, e],
            device_id=(2 * self.s + core, 2 * x + self.yh),
            device_id_type=MESH,
        )

    def height_forward(self, table):
        @pl.loop(0, NCH)
        def _(i):
            for e in range(1, SG):
                self.copyb(i, e).wait_recv()
            own = pl.ds(i * CH, CH)
            spectrum = jnp.concatenate(
                [self.G[s, own].reshape(CH * 64, 128) for s in range(SG)], axis=1
            )
            for x in range(NX):
                lanes = slice(x * 128, (x + 1) * 128)
                shifted = slice(KH + x * 128, KH + (x + 1) * 128)
                both = jnp.concatenate([table[:, lanes], table[:, shifted]], axis=1)
                terms = dot_nn(spectrum, both).reshape(CH, 2, 2, 16, 256)
                real = terms[:, 0, :, :, :128] - terms[:, 1, :, :, 128:]
                imaginary = terms[:, 0, :, :, 128:] + terms[:, 1, :, :, :128]
                for core in range(2):
                    self.K[x, core, own, 0] = real[:, core].astype(BF16)
                    self.K[x, core, own, 1] = imaginary[:, core].astype(BF16)
            for e in range(1, 8):
                self.copyc(i, e).start()
            self.Y0[self.id2, own] = self.K[self.x, self.core, own]

    def modes(self, out):
        @pl.loop(0, NCH)
        def _(i):
            for e in range(1, 8):
                self.copyc(i, e).wait_recv()
        self.y32[...] = self.Y0[...].astype(F32).reshape(BS * 32, 128)
        for part in range(2):
            for k in range(16):
                out[part * BS : (part + 1) * BS, k * 128 : (k + 1) * 128] = self.y32[
                    pl.ds(part * 16 + k, BS, stride=32), :
                ].astype(BF16)

    def copyz(self, e):
        x, core = self.peer2(e)
        return pltpu.make_async_remote_copy(
            src_ref=self.Z0.at[x * 2 + core],
            dst_ref=self.Q.at[self.x, :, :, pl.ds(pl.multiple_of(self.core * 16, 16), 16), :],
            send_sem=self.sems[6].at[e],
            recv_sem=self.sems[7].at[e],
            device_id=(2 * self.s + core, 2 * x + self.yh),
            device_id_type=MESH,
        )

    def from_modes(self, values):
        for q in range(4):
            block = values(q * 512, (q + 1) * 512)
            for part in range(2):
                for j in range(4):
                    self.y32[pl.ds(part * 16 + q * 4 + j, BS, stride=32), :] = block[
                        part * BS : (part + 1) * BS, j * 128 : (j + 1) * 128
                    ]
        self.Z0[...] = self.y32[...].astype(BF16).reshape(8, CG, 2, 16, 128)
        for e in range(1, 8):
            self.copyz(e).start()
        self.Q[self.x, :, :, pl.ds(pl.multiple_of(self.core * 16, 16), 16), :] = self.Z0[self.id2]

    def copyf(self, i, e):
        s = (self.s + e) % SG
        return pltpu.make_async_remote_copy(
            src_ref=self.BK.at[s, pl.ds(i * CH, CH)],
            dst_ref=self.F.at[self.s, pl.ds(i * CH, CH)],
            send_sem=self.sems[8].at[i, e],
            recv_sem=self.sems[9].at[i, e],
            device_id=(2 * s + self.core, self.ci),
            device_id_type=MESH,
        )

    def height_inverse(self, table):
        for e in range(1, 8):
            self.copyz(e).wait_recv()

        @pl.loop(0, NCH)
        def _(i):
            own = pl.ds(i * CH, CH)
            modes = jnp.concatenate([self.Q[x, own].reshape(CH * 64, 128) for x in range(NX)], axis=1)
            for q in range(4):
                rows = slice(q * 256, (q + 1) * 256)
                first = dot_nt(modes, table[rows, :KH]).reshape(CH, 2, 32, 256)
                second = dot_nt(modes, table[rows, KH:]).reshape(CH, 2, 32, 256)
                real = (first[:, 0] + second[:, 1]).astype(BF16)
                imaginary = (first[:, 1] - second[:, 0]).astype(BF16)
                for j in range(2):
                    lanes = slice(j * 128, (j + 1) * 128)
                    self.BK[2 * q + j, own, :32, :] = real[:, :, lanes]
                    self.BK[2 * q + j, own, 32:, :] = imaginary[:, :, lanes]
            for e in range(1, SG):
                self.copyf(i, e).start()
            self.F[self.s, own] = self.BK[self.s, own]

    def copyo(self, out, i, d):
        col, core = self.peer1(d)
        start = self.first_channel(self.ci, self.core) + i * CH
        rows = pl.ds(pl.multiple_of(core * LR, LR), LR)
        return pltpu.make_async_remote_copy(
            src_ref=self.FO.at[col, pl.ds(i * CH, CH), rows, :],
            dst_ref=out.at[pl.ds(start, CH)],
            send_sem=self.sems[10].at[i, d],
            recv_sem=self.sems[11].at[i, d],
            device_id=(2 * self.s + core, col),
            device_id_type=MESH,
        )

    def width_inverse(self, out, table):
        rows = pl.ds(pl.multiple_of(self.core * LR, LR), LR)
        start = self.first_channel(self.ci, self.core)

        @pl.loop(0, NCH)
        def _(i):
            for e in range(1, SG):
                self.copyf(i, e).wait_recv()
            for half in range(CH // 2):
                c = i * CH + 2 * half
                spectrum = jnp.concatenate(
                    [self.F[:, c].reshape(2 * KW, 128), self.F[:, c + 1].reshape(2 * KW, 128)], axis=1
                )
                turned = spectrum.T
                for q in range(4):
                    field = dot_nn(turned, table[:, q * 256 : (q + 1) * 256]).astype(BF16)
                    for j in range(2):
                        self.FO[2 * q + j, pl.ds(c, 2)] = field[:, j * 128 : (j + 1) * 128].reshape(
                            2, 128, 128
                        )
            for d in range(1, 16):
                self.copyo(out, i, d).start()
            out[pl.ds(start + i * CH, CH)] = self.FO[self.ci, pl.ds(i * CH, CH), rows, :]

    def finish(self, src, out):
        @pl.loop(0, NCH)
        def _(i):
            for d in range(1, 16):
                self.copyo(out, i, d).wait_recv()
        self.drain(src, out)

    def drain(self, src, out):
        @pl.loop(0, NCH)
        def _(i):
            for d in range(1, 16):
                self.copy1(src, i, d).wait_send()
                self.copyo(out, i, d).wait_send()
            for e in range(1, 8):
                self.copyb(i, e).wait_send()
                self.copyc(i, e).wait_send()
                self.copyf(i, e).wait_send()
        for e in range(1, 8):
            self.copyz(e).wait_send()


def exchange_scratch():
    dma = pltpu.SemaphoreType.DMA
    pairs = [(NCH, 16), (NCH, 8), (NCH, 8), (8,), (NCH, 8), (NCH, 16)]
    return [
        pltpu.VMEM((8, CG, 2 * LR, LW), BF16),
        pltpu.VMEM((SG, CG, 64, 128), BF16),
        pltpu.VMEM((SG, CG, 64, 128), BF16),
        pltpu.VMEM((NX, 2, CG, 2, 16, 128), BF16),
        pltpu.VMEM((8, CG, 2, 16, 128), BF16),
        pltpu.VMEM((BS * 32, 128), F32),
        pltpu.VMEM((8, CG, 2, 16, 128), BF16),
        pltpu.VMEM((NX, CG, 2, 32, 128), BF16),
        pltpu.VMEM((SG, CG, 64, 128), BF16),
        pltpu.VMEM((SG, CG, 64, 128), BF16),
        pltpu.VMEM((8, CG, 2 * LR, LW), BF16),
    ] + [dma(shape) for shape in pairs for _ in range(2)]


def channel_mean(read):
    total = read(0)
    for c in range(1, C):
        total = total + read(c)
    return total * (1.0 / C)


def norm_rows(field, rows):
    mean = channel_mean(lambda c: field[c, rows, :].astype(F32))

    def square(c):
        centred = field[c, rows, :].astype(F32) - mean
        return centred * centred

    return mean, lax.rsqrt(channel_mean(square) + EPS)


def forward_kernel(
    weather, width, weighted, height, mix_in, bias, mix_out,
    normed, filtered, kept, before_out, hidden_out, slope_out, *scratch
):
    ex = Exchange(scratch)

    @pl.loop(0, LR // 16)
    def _(r):
        rows = pl.ds(pl.multiple_of(r * 16, 16), 16)
        mean, spread = norm_rows(weather, rows)
        for c in range(C):
            normed[c, rows, :] = ((weather[c, rows, :].astype(F32) - mean) * spread).astype(BF16)

    ex.barrier()
    ex.send1(normed)
    ex.width_forward(normed, width)
    ex.height_forward(height)
    ex.modes(kept)

    def mixed(lo, hi):
        before = dot_nn(mix_in[...], kept[:, lo:hi]) + bias[...]
        before_out[:, lo:hi] = before
        cumulative, _ = normal_parts(before)
        hidden = (before * cumulative).astype(BF16)
        hidden_out[:, lo:hi] = hidden
        second = dot_nn(mix_out[...], hidden)
        slope = jnp.tanh(second * (1.0 / THRESHOLD))
        slope_out[:, lo:hi] = slope
        return second - THRESHOLD * slope

    ex.from_modes(mixed)
    ex.height_inverse(height)
    ex.width_inverse(filtered, weighted)
    ex.finish(normed, filtered)


def backward_kernel(
    weather, grad_sum, width, weighted, height, mix_in_t, mix_out_t, kept, before, hidden, slope,
    grad_weather, grad_in, grad_out, grad_bias, low, filtered, grads, gate, *scratch
):
    ex = Exchange(scratch)

    @pl.loop(0, LR // 16)
    def _(r):
        rows = pl.ds(pl.multiple_of(r * 16, 16), 16)
        for c in range(C):
            low[c, rows, :] = grad_sum[c, rows, :].astype(BF16)

    ex.barrier()
    ex.send1(low)
    ex.width_forward(low, weighted)
    ex.height_forward(height)
    ex.modes(grads)

    def mixed(lo, hi):
        factor = slope[:, lo:hi]
        second = (grads[:, lo:hi].astype(F32) * (factor * factor)).astype(BF16)
        grads[:, lo:hi] = second
        back = dot_nn(mix_out_t[...], second)
        values = before[:, lo:hi]
        cumulative, density = normal_parts(values)
        gated = (back * (cumulative + values * density)).astype(BF16)
        gate[:, lo:hi] = gated
        return dot_nn(mix_in_t[...], gated)

    ex.from_modes(mixed)
    grad_out[...] = dot_nt(hidden[...], grads[...])
    grad_in[...] = dot_nt(kept[...], gate[...])
    grad_bias[...] = jnp.sum(gate[...].astype(F32), axis=1, keepdims=True)
    ex.height_inverse(height)
    ex.width_inverse(filtered, width)
    ex.finish(low, filtered)

    @pl.loop(0, LR // 16)
    def _(r):
        rows = pl.ds(pl.multiple_of(r * 16, 16), 16)
        mean, spread = norm_rows(weather, rows)

        def total(c):
            return grad_sum[c, rows, :] + filtered[c, rows, :].astype(F32)

        def normal(c):
            return (weather[c, rows, :].astype(F32) - mean) * spread

        mean_grad = channel_mean(total)
        mean_cross = channel_mean(lambda c: total(c) * normal(c))
        for c in range(C):
            inner = total(c) - mean_grad - normal(c) * mean_cross
            grad_weather[c, rows, :] = (grad_sum[c, rows, :] + spread * inner).astype(BF16)


TR = 16
TN = TR * LW
CHUNK = 512


def token_kernel(
    weather, normed_in, filtered, cotangent, pin, pin_t, pout, pout_t,
    output, grad_sum, acc_in, acc_out, s32, x32, c32, g32, normal_low, cot_low
):
    step = pl.program_id(0)

    @pl.when(step == 0)
    def _():
        acc_in[...] = jnp.zeros_like(acc_in)
        acc_out[...] = jnp.zeros_like(acc_out)

    def at(c):
        return slice(c * TR, (c + 1) * TR)

    total = jnp.zeros((TR, LW), F32)
    for c in range(C):
        value = weather[c].astype(F32) + normed_in[c].astype(F32) + filtered[c].astype(F32)
        s32[at(c), :] = value
        total = total + value
        c32[at(c), :] = cotangent[c].astype(F32)
    mean = total * (1.0 / C)

    def square(c):
        centred = s32[at(c), :] - mean
        return centred * centred

    spread = lax.rsqrt(channel_mean(square) + EPS)
    for c in range(C):
        x32[at(c), :] = (s32[at(c), :] - mean) * spread
    for j in range(TR):
        lanes = slice(j * LW, (j + 1) * LW)
        normal_low[:, lanes] = x32[pl.ds(j, C, stride=TR), :].astype(BF16)
        cot_low[:, lanes] = c32[pl.ds(j, C, stride=TR), :].astype(BF16)

    @pl.loop(0, TN // CHUNK)
    def _(q):
        lanes = pl.ds(pl.multiple_of(q * CHUNK, CHUNK), CHUNK)
        normal = normal_low[:, lanes]
        cot = cot_low[:, lanes]
        before = dot_nn(pin_t[...], normal)
        cumulative, density = normal_parts(before)
        hidden = (before * cumulative).astype(BF16)
        back_hidden = dot_nn(pout[...], cot)
        back_before = (back_hidden * (cumulative + before * density)).astype(BF16)
        out = dot_nn(pout_t[...], hidden)
        back_normed = dot_nn(pin[...], back_before)
        acc_out[...] += dot_nt(hidden, cot)
        acc_in[...] += dot_nt(back_before, normal)
        for j in range(CHUNK // LW):
            sl = slice(j * LW, (j + 1) * LW)
            where = pl.ds(q * (CHUNK // LW) + j, C, stride=TR)
            s32[where, :] += out[:, sl]
            g32[where, :] = back_normed[:, sl]

    for c in range(C):
        output[c] = s32[at(c), :].astype(BF16)
    mean_grad = channel_mean(lambda c: g32[at(c), :])
    mean_cross = channel_mean(lambda c: g32[at(c), :] * x32[at(c), :])
    for c in range(C):
        inner = g32[at(c), :] - mean_grad - x32[at(c), :] * mean_cross
        grad_sum[c] = c32[at(c), :] + spread * inner


def vmem():
    return pl.BlockSpec(memory_space=pltpu.VMEM)


def forward_call(weather, width, weighted, height, mix_in, bias, mix_out):
    shape = jax.ShapeDtypeStruct
    return pl.pallas_call(
        forward_kernel,
        out_shape=(
            shape((C, LR, LW), BF16),
            shape((C, LR, LW), BF16),
            shape((C, MODES), BF16),
            shape((C, MODES), F32),
            shape((C, MODES), BF16),
            shape((C, MODES), F32),
        ),
        in_specs=[vmem()] * 7,
        out_specs=[vmem()] * 6,
        scratch_shapes=exchange_scratch(),
        compiler_params=pltpu.CompilerParams(
            collective_id=0, has_side_effects=True, vmem_limit_bytes=60 << 20
        ),
        name="spectral_forward",
    )(weather, width, weighted, height, mix_in, bias, mix_out)


def backward_call(*args):
    shape = jax.ShapeDtypeStruct
    return pl.pallas_call(
        backward_kernel,
        out_shape=(
            shape((C, LR, LW), BF16),
            shape((C, C), F32),
            shape((C, C), F32),
            shape((C, 1), F32),
        ),
        in_specs=[vmem()] * 11,
        out_specs=[vmem()] * 4,
        scratch_shapes=[
            pltpu.VMEM((C, LR, LW), BF16),
            pltpu.VMEM((C, LR, LW), BF16),
            pltpu.VMEM((C, MODES), BF16),
            pltpu.VMEM((C, MODES), BF16),
        ]
        + exchange_scratch(),
        compiler_params=pltpu.CompilerParams(
            collective_id=1, has_side_effects=True, vmem_limit_bytes=63 << 20
        ),
        name="spectral_backward",
    )(*args)


def token_call(weather, normed_in, filtered, cotangent, pin, pin_t, pout, pout_t):
    shape = jax.ShapeDtypeStruct
    block = pl.BlockSpec((C, TR, LW), lambda i: (0, i, 0))

    def whole(*dims):
        return pl.BlockSpec(dims, lambda i: (0,) * len(dims))

    return pl.pallas_call(
        token_kernel,
        grid=(LR // TR,),
        out_shape=(
            shape((C, LR, LW), BF16),
            shape((C, LR, LW), F32),
            shape((HID, C), F32),
            shape((HID, C), F32),
        ),
        in_specs=[block] * 4 + [whole(C, HID), whole(HID, C), whole(HID, C), whole(C, HID)],
        out_specs=[block, block, whole(HID, C), whole(HID, C)],
        scratch_shapes=[pltpu.VMEM((C * TR, LW), F32)] * 4 + [pltpu.VMEM((C, TN), BF16)] * 2,
        compiler_params=pltpu.CompilerParams(vmem_limit_bytes=60 << 20),
        name="token_block",
    )(weather, normed_in, filtered, cotangent, pin, pin_t, pout, pout_t)


def mixing(weights):
    real, imaginary = weights[0].T, weights[1].T
    return jnp.concatenate(
        [
            jnp.concatenate([real, -imaginary], axis=1),
            jnp.concatenate([imaginary, real], axis=1),
        ],
        axis=0,
    )


def complex_grad(pairs):
    return jnp.stack(
        [
            pairs[:BS, :BS] + pairs[BS:, BS:],
            pairs[:BS, BS:] - pairs[BS:, :BS],
        ]
    )


def body(weather, cotangent, spectral_in, spectral_bias, spectral_out, project_in, project_out):
    width, weighted, height = tables()
    block = lax.axis_index("col") % 2
    mix_in = mixing(lax.dynamic_index_in_dim(spectral_in, block, axis=1, keepdims=False))
    mix_out = mixing(lax.dynamic_index_in_dim(spectral_out, block, axis=1, keepdims=False))
    bias = lax.dynamic_index_in_dim(spectral_bias, block, axis=1, keepdims=False).reshape(C, 1)
    normed, filtered, kept, before, hidden, slope = forward_call(
        weather, width, weighted, height, mix_in, bias, mix_out
    )
    output, grad_sum, acc_in, acc_out = token_call(
        weather, normed, filtered, cotangent, project_in, project_in.T, project_out, project_out.T
    )
    early = lax.psum(jnp.stack([acc_in, acc_out]), ("row", "col"))
    grad_weather, grad_first, grad_second, grad_bias = backward_call(
        weather, grad_sum, width, weighted, height, mix_in.T, mix_out.T, kept, before, hidden, slope
    )
    late = jnp.concatenate(
        [
            complex_grad(grad_first).reshape(-1),
            complex_grad(grad_second).reshape(-1),
            grad_bias.reshape(-1),
        ]
    )
    slots = jnp.where(jnp.arange(2)[:, None] == block, late[None, :], 0.0)
    late = lax.psum(slots, ("row", "col"))
    size = 2 * BS * BS
    grad_spectral_in = late[:, :size].reshape(2, 2, BS, BS).transpose(1, 0, 2, 3)
    grad_spectral_out = late[:, size : 2 * size].reshape(2, 2, BS, BS).transpose(1, 0, 2, 3)
    grad_spectral_bias = late[:, 2 * size :].reshape(2, 2, BS).transpose(1, 0, 2)
    return (
        output,
        grad_weather,
        early[0].T / H,
        early[1] / H,
        grad_spectral_in / H,
        grad_spectral_out / H,
        grad_spectral_bias / H,
    )


def solution(mesh):
    in_specs = (P(None, "row", "col"), P(None, "row", "col"), P(), P(), P(), P(), P())
    out_specs = (P(None, "row", "col"), P(None, "row", "col"), P(), P(), P(), P(), P())
    return jax.shard_map(body, mesh=mesh, in_specs=in_specs, out_specs=out_specs, check_vma=False)
```

time: 841 us -> 535 us (0.64)
  Pallas kernels: 0 us -> 340 us
  matrix products: 248 us -> 0 us
  blocking collectives: 241 us -> 0 us
  other arithmetic: 79.1 us -> 12.7 us
  local copies, waits for them, and re-layouts: 76.8 us -> 16.2 us
  starting transfers between devices: 37.4 us -> 0.04 us
  waiting for transfers between devices: 136 us -> 151 us
    pallas_call x0 -> x3, Pallas kernels: none -> 340 us  [the longest x1 148 us: backward_call(): pl.pallas_call(backward_kernel, out_shape=(shape((C, LR, LW), BF16), shap...]
    dot_general x42 -> x0, matrix products: 226 us -> none  [product(): return jnp.einsum(form, left, right, preferred_element_type=jnp.float32)]
    all_to_all x3 -> x0, blocking collectives: 139 us -> none  [the longest x2 85.2 us: to_columns(): lax.all_to_all(field_part, 'col', split_axis=1, concat_axis=2, tiled=True)]
    psum x1 -> x0, blocking collectives: 102 us -> none  [body(): lax.psum((grad_in, grad_out, grad_first, grad_second, grad_bias), ('row',...]
    psum x1, waiting for transfers between devices: 69.6 us -> 151 us  [body(): early = lax.psum(jnp.stack([acc_in, acc_out]), ('row', 'col'))]
    all_to_all x5 -> x0, waiting for transfers between devices: 66.6 us -> none  [the longest x2 35.1 us: to_modes(): lax.all_to_all(spectrum, ('row', 'col'), split_axis=1, concat_axis=0, til...]
    all_to_all x5 -> x0, starting transfers between devices: 37.2 us -> none  [the longest x2 20 us: to_modes(): lax.all_to_all(spectrum, ('row', 'col'), split_axis=1, concat_axis=0, til...]
    convert_element_type x7 -> x0, local copies, waits for them, and re-layouts: 33.3 us -> none  [the longest x2 12.4 us: width_inverse(): return summed.astype(jnp.bfloat16)]
  transfers between devices with their start and end apart: 6 -> 1, of which waited for: 5 -> 1; matrix products, arithmetic and copies ran while one was open for 6% -> 0% of each run, Pallas kernels for 0% -> 0%
where the time goes in v1:
time: 535 us; the launch traced here: 534 us
  Pallas kernels  340 us (64%)
  waiting for transfers between devices  151 us (28%)
  local copies, waits for them, and re-layouts  16.2 us (3%)
  between operations  14.2 us (3%)
  other arithmetic  12.7 us (2%)
    psum x1, waiting for transfers between devices, body(): early = lax.psum(jnp.stack([acc_in, acc_out]), ('row', 'col'))  151 us
    pallas_call x1, Pallas kernels, backward_call(): pl.pallas_call(backward_kernel, out_shape=(shape((C, LR, LW), BF16), shap...  148 us
    pallas_call x1, Pallas kernels, forward_call(): pl.pallas_call(forward_kernel, out_shape=(shape((C, LR, LW), BF16), shape...  145 us
    pallas_call x1, Pallas kernels, token_call(): pl.pallas_call(token_kernel, grid=(LR // TR,), out_shape=(shape((C, LR, L...  46.6 us
    unnamed x18, local copies, waits for them, and re-layouts  11.6 us
  transfers between devices with their start and end apart: 1, of which 1 were waited for; matrix products, arithmetic and copies ran while one was open for 0% of the time, Pallas kernels for 0%

profile of v1, /device:TPU:1, one launch (start us, length us, event | category | flops | bytes accessed | tf_op | source)
XLA Modules:
  0.0 534.4 jit_solution(5718131674317917152)
XLA Ops:
  7.2 0.0 copy-start
  7.2 0.0 copy-start.2
  7.2 0.0 all-reduce.3.cloned.1.call-start
  7.3 0.6 copy-done
  7.9 0.8 reshape.58.bias
  8.7 0.8 dynamic-slice_bitcast_fusion.1
  9.5 0.8 fusion.5
  10.2 0.7 fusion.3
  11.0 0.7 copy.25.mix_out
  11.7 0.7 fusion.4
  12.4 0.7 copy.23.mix_in
  13.2 1.9 copy.26
  15.1 0.0 copy-done.2
  15.1 0.9 copy.27.pout
  16.0 145.0 %spectral_forward.1 = (bf16[192,64,128]{2,1,0:T(8,128)(2,1)}, bf16[192,64,128]{2,1,0:T(8,128)(2,1)}, bf16[192,2048]{1,0:T(8,128)(2,1)}, f32[192,2048]{1,0:T(8,12...) custom-call(bf16[192,64,128]{2,1,0:T(8,128)(2,1)} %weather.5, bf16[512,1024]{1,0:T(8,128)(2,1)} %constant.48.width, ...), custom_call_target="tpu_custom_call" | custom-call | tf_op jit(solution)/shard_map/spectral_forward/pallas_call | solution.py:519
  161.0 46.6 %token_block.1 = (bf16[192,64,128]{2,1,0:T(8,128)(2,1)}, f32[192,64,128]{2,1,0:T(8,128)}, f32[768,192]{1,0:T(8,128)}, f32[768,192]{1,0:T(8,128)}) custom-call(bf16[192,64,128]{2,1,0:T(8,128)(2,1)} %weather.5, bf16[192,64,128]{2,1,0:T(8,128)(2,1)} %get-tuple-element.21.normed_in, bf16[192,64,128]{2,1,0:T(8,128)(2,1)} %get-tuple-element.22.filtered, ...), custom_call_target="tpu_custom_call" | custom-call | tf_op jit(solution)/shard_map/token_block/pallas_call | solution.py:572
  207.6 148.2 %spectral_backward.1 = (bf16[192,64,128]{2,1,0:T(8,128)(2,1)}, f32[192,192]{1,0:T(8,128)}, f32[192,192]{1,0:T(8,128)}, f32[192,1]{1,0:T(8,128)}) custom-call(bf16[192,64,128]{2,1,0:T(8,128)(2,1)} %weather.5, f32[192,64,128]{2,1,0:T(8,128)} %get-tuple-element.24.grad_sum, bf16[512,1024]{1,0:T(8,128)(2,1)} %constant.48.width, ...), custom_call_target="tpu_custom_call" | custom-call | tf_op jit(solution)/shard_map/spectral_backward/pallas_call | solution.py:541
  355.8 0.0 copy-start.3
  355.8 0.0 copy-start.4
  355.8 1.2 add_bitcast_fusion.1
  357.0 0.1 reshape.55
  357.1 1.1 add_bitcast_fusion
  358.2 0.1 reshape.56
  358.4 1.0 reduce.1
  359.4 0.9 broadcast_select_fusion
  360.3 0.0 copy-done.3
  360.3 0.0 copy-done.4
  360.3 1.2 pad_maximum_fusion
  361.5 0.0 all-reduce.3.cloned.1.call-update
  361.6 151.4 %all-reduce.3.cloned.1.call-done = (f32[2,768,192]{2,1,0:T(8,128)}, f32[2,37056]{1,0:T(2,128)}) async-done(((f32[2,768,192]{2,1,0:T(8,128)}, f32[2,37056]{1,0:T(2,128)}), (f32[2,768,192]{2,1,0:T(8,128)}, f32[2,37056]{1,0:T(2,128)})) %all-reduce.3.cloned.1.call-update) | async-done | bytes 1476112 | tf_op jit(solution)/shard_map/psum | solution.py:621
  512.9 0.7 slice_multiply_fusion.4
  513.6 1.8 slice_multiply_fusion.2
  515.4 2.6 fusion
  518.0 0.0 copy-start.1
  518.0 2.3 copy.29
  520.4 0.1 div.54
  520.5 0.6 copy.32
  521.0 1.1 div.50
  522.1 0.7 copy.31
  522.8 0.2 div.47
  523.0 0.7 copy.30
  523.7 2.2 copy.28
  525.9 0.0 copy-done.1
  525.9 1.7 copy.36
  (5 shorter events, 0.1 us)
Async XLA Ops:
  7.2 0.7 copy-start
  7.2 7.9 %copy-start.2 = (bf16[768,192]{0,1:T(8,128)(2,1)S(1)}, bf16[768,192]{0,1:T(8,128)(2,1)}, u32[]{:S(2)}) copy-start(bf16[768,192]{0,1:T(8,128)(2,1)} %param.16) | copy-start | bytes 884740
  7.2 505.8 %all-reduce.3.cloned.1.call-start = ((), (), s32[]{:S(2)}) async-start(), calls=%async_computation | async-start | bytes 3739648 | tf_op jit(solution)/shard_map/psum | solution.py:621
  355.8 4.5 copy-start.3
  355.8 4.5 copy-start.4
  518.0 7.9 %copy-start.1 = (bf16[192,64,128]{2,1,0:T(8,128)(2,1)S(1)}, bf16[192,64,128]{2,1,0:T(8,128)(2,1)}, u32[]{:S(2)}) copy-start(bf16[192,64,128]{2,1,0:T(8,128)(2,1)} %get-tuple-element.79) | copy-start | bytes 9437188
Sparse Core Ops, SparseCore 0:
  361.7 151.2 all-reduce.2

commit v2 on v1

--- a/solution.py
+++ b/solution.py
@@ -334,6 +334,118 @@
     ] + [dma(shape) for shape in pairs for _ in range(2)]
 
 
+class Reduction:
+    def __init__(self, ex, scratch):
+        self.ex = ex
+        self.src, self.ra, self.t1, self.rb, self.t2, self.rc, self.out = scratch[:7]
+        self.sems = scratch[7:17]
+
+    def copy_a(self):
+        ex = self.ex
+        return pltpu.make_async_remote_copy(
+            src_ref=self.src.at[1 - ex.core],
+            dst_ref=self.ra,
+            send_sem=self.sems[0],
+            recv_sem=self.sems[1],
+            device_id=(2 * ex.s + 1 - ex.core, ex.ci),
+            device_id_type=MESH,
+        )
+
+    def copy_b(self, e):
+        ex = self.ex
+        s = (ex.s + e) % SG
+        return pltpu.make_async_remote_copy(
+            src_ref=self.t1.at[s],
+            dst_ref=self.rb.at[ex.s],
+            send_sem=self.sems[2].at[e],
+            recv_sem=self.sems[3].at[e],
+            device_id=(2 * s + ex.core, ex.ci),
+            device_id_type=MESH,
+        )
+
+    def copy_c(self, e):
+        ex = self.ex
+        return pltpu.make_async_remote_copy(
+            src_ref=self.t2,
+            dst_ref=self.rc.at[ex.ci],
+            send_sem=self.sems[4].at[e],
+            recv_sem=self.sems[5].at[e],
+            device_id=(ex.ri, (ex.ci + e) % 8),
+            device_id_type=MESH,
+        )
+
+    def copy_d(self, e):
+        ex = self.ex
+        return pltpu.make_async_remote_copy(
+            src_ref=self.out.at[ex.core, ex.s],
+            dst_ref=self.out.at[ex.core, ex.s],
+            send_sem=self.sems[6].at[e],
+            recv_sem=self.sems[7].at[e],
+            device_id=(2 * ((ex.s + e) % SG) + ex.core, ex.ci),
+            device_id_type=MESH,
+        )
+
+    def copy_e(self):
+        ex = self.ex
+        return pltpu.make_async_remote_copy(
+            src_ref=self.out.at[ex.core],
+            dst_ref=self.out.at[ex.core],
+            send_sem=self.sems[8],
+            recv_sem=self.sems[9],
+            device_id=(2 * ex.s + 1 - ex.core, ex.ci),
+            device_id_type=MESH,
+        )
+
+    def round(self, number):
+        ex = self.ex
+        if number == 0:
+            self.copy_a().start()
+        elif number == 1:
+            self.copy_a().wait_recv()
+            self.t1[...] = self.src[ex.core] + self.ra[...]
+            for e in range(1, 8):
+                self.copy_b(e).start()
+            self.rb[ex.s] = self.t1[ex.s]
+        elif number == 2:
+            for e in range(1, 8):
+                self.copy_b(e).wait_recv()
+            self.t2[...] = jnp.sum(self.rb[...], axis=0)
+            for e in range(1, 8):
+                self.copy_c(e).start()
+            self.rc[ex.ci] = self.t2[...]
+        elif number == 3:
+            for e in range(1, 8):
+                self.copy_c(e).wait_recv()
+            self.out[ex.core, ex.s] = jnp.sum(self.rc[...], axis=0) * (1.0 / H)
+            for e in range(1, 8):
+                self.copy_d(e).start()
+        elif number == 4:
+            for e in range(1, 8):
+                self.copy_d(e).wait_recv()
+            self.copy_e().start()
+        else:
+            self.copy_e().wait_recv()
+            self.copy_a().wait_send()
+            self.copy_e().wait_send()
+            for e in range(1, 8):
+                self.copy_b(e).wait_send()
+                self.copy_c(e).wait_send()
+                self.copy_d(e).wait_send()
+
+
+def reduction_scratch(rows, lanes, source):
+    dma = pltpu.SemaphoreType.DMA
+    part = pltpu.VMEM((8, rows, lanes), F32)
+    buffers = [pltpu.VMEM((2, 8, rows, lanes), F32)] if source else []
+    return (
+        buffers
+        + [part, part, part, pltpu.VMEM((rows, lanes), F32), part, pltpu.VMEM((2, 8, rows, lanes), F32)]
+        + [dma] * 2
+        + [dma((8,))] * 6
+        + [dma] * 2
+    )
+
+
 def channel_mean(read):
     total = read(0)
     for c in range(1, C):
@@ -352,7 +464,7 @@
 
 
 def forward_kernel(
-    weather, width, weighted, height, mix_in, bias, mix_out,
+    weather, width, weighted, height, spectral_in, bias, spectral_out,
     normed, filtered, kept, before_out, hidden_out, slope_out, *scratch
 ):
     ex = Exchange(scratch)
@@ -370,13 +482,30 @@
     ex.height_forward(height)
     ex.modes(kept)
 
+    a_re, a_im = spectral_in[0, ex.yh], spectral_in[1, ex.yh]
+    b_re, b_im = spectral_out[0, ex.yh], spectral_out[1, ex.yh]
+
     def mixed(lo, hi):
-        before = dot_nn(mix_in[...], kept[:, lo:hi]) + bias[...]
+        real, imaginary = kept[:BS, lo:hi], kept[BS:, lo:hi]
+        before = jnp.concatenate(
+            [
+                dot_tn(a_re, real) - dot_tn(a_im, imaginary) + bias[0, ex.yh],
+                dot_tn(a_re, imaginary) + dot_tn(a_im, real) + bias[1, ex.yh],
+            ],
+            axis=0,
+        )
         before_out[:, lo:hi] = before
         cumulative, _ = normal_parts(before)
         hidden = (before * cumulative).astype(BF16)
         hidden_out[:, lo:hi] = hidden
-        second = dot_nn(mix_out[...], hidden)
+        real, imaginary = hidden[:BS], hidden[BS:]
+        second = jnp.concatenate(
+            [
+                dot_tn(b_re, real) - dot_tn(b_im, imaginary),
+                dot_tn(b_re, imaginary) + dot_tn(b_im, real),
+            ],
+            axis=0,
+        )
         slope = jnp.tanh(second * (1.0 / THRESHOLD))
         slope_out[:, lo:hi] = slope
         return second - THRESHOLD * slope
@@ -388,10 +517,14 @@
 
 
 def backward_kernel(
-    weather, grad_sum, width, weighted, height, mix_in_t, mix_out_t, kept, before, hidden, slope,
-    grad_weather, grad_in, grad_out, grad_bias, low, filtered, grads, gate, *scratch
+    weather, grad_sum, token_grads, width, weighted, height, spectral_in, spectral_out,
+    kept, before, hidden, slope,
+    grad_weather, grad_pin, grad_pout, grad_in, grad_out, grad_bias,
+    low, filtered, grads, gate, *scratch
 ):
     ex = Exchange(scratch)
+    first = Reduction(ex, (token_grads,) + scratch[23:39])
+    other = Reduction(ex, scratch[39:56])
 
     @pl.loop(0, LR // 16)
     def _(r):
@@ -400,29 +533,78 @@
             low[c, rows, :] = grad_sum[c, rows, :].astype(BF16)
 
     ex.barrier()
+    first.round(0)
     ex.send1(low)
     ex.width_forward(low, weighted)
+    first.round(1)
     ex.height_forward(height)
+    first.round(2)
     ex.modes(grads)
+    a_re, a_im = spectral_in[0, ex.yh], spectral_in[1, ex.yh]
+    b_re, b_im = spectral_out[0, ex.yh], spectral_out[1, ex.yh]
 
     def mixed(lo, hi):
         factor = slope[:, lo:hi]
         second = (grads[:, lo:hi].astype(F32) * (factor * factor)).astype(BF16)
         grads[:, lo:hi] = second
-        back = dot_nn(mix_out_t[...], second)
+        real, imaginary = second[:BS], second[BS:]
+        back = jnp.concatenate(
+            [
+                dot_nn(b_re, real) + dot_nn(b_im, imaginary),
+                dot_nn(b_re, imaginary) - dot_nn(b_im, real),
+            ],
+            axis=0,
+        )
         values = before[:, lo:hi]
         cumulative, density = normal_parts(values)
         gated = (back * (cumulative + values * density)).astype(BF16)
         gate[:, lo:hi] = gated
-        return dot_nn(mix_in_t[...], gated)
+        real, imaginary = gated[:BS], gated[BS:]
+        return jnp.concatenate(
+            [
+                dot_nn(a_re, real) + dot_nn(a_im, imaginary),
+                dot_nn(a_re, imaginary) - dot_nn(a_im, real),
+            ],
+            axis=0,
+        )
 
     ex.from_modes(mixed)
-    grad_out[...] = dot_nt(hidden[...], grads[...])
-    grad_in[...] = dot_nt(kept[...], gate[...])
-    grad_bias[...] = jnp.sum(gate[...].astype(F32), axis=1, keepdims=True)
+    first.round(3)
+    sums = other.src
+    sums[...] = jnp.zeros_like(sums)
+    low_half, high_half = slice(0, BS), slice(BS, 2 * BS)
+    for base, left, right in ((0, kept, gate), (2, hidden, grads)):
+        real = dot_nt(left[low_half, :], right[low_half, :]) + dot_nt(
+            left[high_half, :], right[high_half, :]
+        )
+        imaginary = dot_nt(left[low_half, :], right[high_half, :]) - dot_nt(
+            left[high_half, :], right[low_half, :]
+        )
+        for part, value in enumerate((real, imaginary)):
+            at = 2 * (base + part)
+            sums[ex.yh, at : at + 2, :, :BS] = value.reshape(2, 48, BS)
+    for part in range(2):
+        value = jnp.sum(gate[part * BS : (part + 1) * BS, :].astype(F32), axis=1, keepdims=True)
+        sums[ex.yh, 2 * part : 2 * part + 2, :, BS : BS + 1] = value.reshape(2, 48, 1)
+    other.round(0)
     ex.height_inverse(height)
+    first.round(4)
+    other.round(1)
     ex.width_inverse(filtered, width)
+    other.round(2)
+    first.round(5)
+    other.round(3)
+    grad_pin[...] = first.out[0].reshape(C, HID)
+    grad_pout[...] = first.out[1].reshape(C, HID).T
+    other.round(4)
     ex.finish(low, filtered)
+    other.round(5)
+    for block in range(2):
+        for part in range(2):
+            for base, target in ((0, grad_in), (2, grad_out)):
+                at = 2 * (base + part)
+                target[part, block] = other.out[block, at : at + 2, :, :BS].reshape(BS, BS)
+            grad_bias[part, block] = other.out[block, 2 * part : 2 * part + 2, :, BS : BS + 1].reshape(BS, 1)
 
     @pl.loop(0, LR // 16)
     def _(r):
@@ -448,8 +630,8 @@
 
 
 def token_kernel(
-    weather, normed_in, filtered, cotangent, pin, pin_t, pout, pout_t,
-    output, grad_sum, acc_in, acc_out, s32, x32, c32, g32, normal_low, cot_low
+    weather, normed_in, filtered, cotangent, pin, pout,
+    output, grad_sum, grads, acc_in, acc_out, pin_t, pout_t, s32, x32, c32, g32, normal_low, cot_low
 ):
     step = pl.program_id(0)
 
@@ -457,6 +639,8 @@
     def _():
         acc_in[...] = jnp.zeros_like(acc_in)
         acc_out[...] = jnp.zeros_like(acc_out)
+        pin_t[...] = pin[...].T
+        pout_t[...] = pout[...].T
 
     def at(c):
         return slice(c * TR, (c + 1) * TR)
@@ -509,12 +693,17 @@
         inner = g32[at(c), :] - mean_grad - x32[at(c), :] * mean_cross
         grad_sum[c] = c32[at(c), :] + spread * inner
 
+    @pl.when(step == pl.num_programs(0) - 1)
+    def _():
+        grads[0] = acc_in[...].T.reshape(8, 24, HID)
+        grads[1] = acc_out[...].T.reshape(8, 24, HID)
+
 
 def vmem():
     return pl.BlockSpec(memory_space=pltpu.VMEM)
 
 
-def forward_call(weather, width, weighted, height, mix_in, bias, mix_out):
+def forward_call(*args):
     shape = jax.ShapeDtypeStruct
     return pl.pallas_call(
         forward_kernel,
@@ -533,7 +722,7 @@
             collective_id=0, has_side_effects=True, vmem_limit_bytes=60 << 20
         ),
         name="spectral_forward",
-    )(weather, width, weighted, height, mix_in, bias, mix_out)
+    )(*args)
 
 
 def backward_call(*args):
@@ -542,19 +731,23 @@
         backward_kernel,
         out_shape=(
             shape((C, LR, LW), BF16),
-            shape((C, C), F32),
-            shape((C, C), F32),
-            shape((C, 1), F32),
+            shape((C, HID), F32),
+            shape((HID, C), F32),
+            shape((2, NB, BS, BS), F32),
+            shape((2, NB, BS, BS), F32),
+            shape((2, NB, BS, 1), F32),
         ),
-        in_specs=[vmem()] * 11,
-        out_specs=[vmem()] * 4,
+        in_specs=[vmem()] * 12,
+        out_specs=[vmem()] * 6,
         scratch_shapes=[
             pltpu.VMEM((C, LR, LW), BF16),
             pltpu.VMEM((C, LR, LW), BF16),
             pltpu.VMEM((C, MODES), BF16),
             pltpu.VMEM((C, MODES), BF16),
         ]
-        + exchange_scratch(),
+        + exchange_scratch()
+        + reduction_scratch(24, HID, False)
+        + reduction_scratch(48, 128, True),
         compiler_params=pltpu.CompilerParams(
             collective_id=1, has_side_effects=True, vmem_limit_bytes=63 << 20
         ),
@@ -562,7 +755,7 @@
     )(*args)
 
 
-def token_call(weather, normed_in, filtered, cotangent, pin, pin_t, pout, pout_t):
+def token_call(*args):
     shape = jax.ShapeDtypeStruct
     block = pl.BlockSpec((C, TR, LW), lambda i: (0, i, 0))
 
@@ -575,74 +768,40 @@
         out_shape=(
             shape((C, LR, LW), BF16),
             shape((C, LR, LW), F32),
-            shape((HID, C), F32),
-            shape((HID, C), F32),
+            shape((2, 8, 24, HID), F32),
         ),
-        in_specs=[block] * 4 + [whole(C, HID), whole(HID, C), whole(HID, C), whole(C, HID)],
-        out_specs=[block, block, whole(HID, C), whole(HID, C)],
-        scratch_shapes=[pltpu.VMEM((C * TR, LW), F32)] * 4 + [pltpu.VMEM((C, TN), BF16)] * 2,
+        in_specs=[block] * 4 + [whole(C, HID), whole(HID, C)],
+        out_specs=[block, block, whole(2, 8, 24, HID)],
+        scratch_shapes=[pltpu.VMEM((HID, C), F32)] * 2
+        + [pltpu.VMEM((HID, C), BF16), pltpu.VMEM((C, HID), BF16)]
+        + [pltpu.VMEM((C * TR, LW), F32)] * 4
+        + [pltpu.VMEM((C, TN), BF16)] * 2,
         compiler_params=pltpu.CompilerParams(vmem_limit_bytes=60 << 20),
         name="token_block",
-    )(weather, normed_in, filtered, cotangent, pin, pin_t, pout, pout_t)
-
-
-def mixing(weights):
-    real, imaginary = weights[0].T, weights[1].T
-    return jnp.concatenate(
-        [
-            jnp.concatenate([real, -imaginary], axis=1),
-            jnp.concatenate([imaginary, real], axis=1),
-        ],
-        axis=0,
-    )
-
-
-def complex_grad(pairs):
-    return jnp.stack(
-        [
-            pairs[:BS, :BS] + pairs[BS:, BS:],
-            pairs[:BS, BS:] - pairs[BS:, :BS],
-        ]
-    )
+    )(*args)
 
 
 def body(weather, cotangent, spectral_in, spectral_bias, spectral_out, project_in, project_out):
     width, weighted, height = tables()
-    block = lax.axis_index("col") % 2
-    mix_in = mixing(lax.dynamic_index_in_dim(spectral_in, block, axis=1, keepdims=False))
-    mix_out = mixing(lax.dynamic_index_in_dim(spectral_out, block, axis=1, keepdims=False))
-    bias = lax.dynamic_index_in_dim(spectral_bias, block, axis=1, keepdims=False).reshape(C, 1)
+    bias = spectral_bias.reshape(2, NB, BS, 1)
     normed, filtered, kept, before, hidden, slope = forward_call(
-        weather, width, weighted, height, mix_in, bias, mix_out
+        weather, width, weighted, height, spectral_in, bias, spectral_out
     )
-    output, grad_sum, acc_in, acc_out = token_call(
-        weather, normed, filtered, cotangent, project_in, project_in.T, project_out, project_out.T
+    output, grad_sum, token_grads = token_call(
+        weather, normed, filtered, cotangent, project_in, project_out
     )
-    early = lax.psum(jnp.stack([acc_in, acc_out]), ("row", "col"))
-    grad_weather, grad_first, grad_second, grad_bias = backward_call(
-        weather, grad_sum, width, weighted, height, mix_in.T, mix_out.T, kept, before, hidden, slope
+    grad_weather, grad_pin, grad_pout, grad_in, grad_out, grad_bias = backward_call(
+        weather, grad_sum, token_grads, width, weighted, height, spectral_in, spectral_out,
+        kept, before, hidden, slope,
     )
-    late = jnp.concatenate(
-        [
-            complex_grad(grad_first).reshape(-1),
-            complex_grad(grad_second).reshape(-1),
-            grad_bias.reshape(-1),
-        ]
-    )
-    slots = jnp.where(jnp.arange(2)[:, None] == block, late[None, :], 0.0)
-    late = lax.psum(slots, ("row", "col"))
-    size = 2 * BS * BS
-    grad_spectral_in = late[:, :size].reshape(2, 2, BS, BS).transpose(1, 0, 2, 3)
-    grad_spectral_out = late[:, size : 2 * size].reshape(2, 2, BS, BS).transpose(1, 0, 2, 3)
-    grad_spectral_bias = late[:, 2 * size :].reshape(2, 2, BS).transpose(1, 0, 2)
     return (
         output,
         grad_weather,
-        early[0].T / H,
-        early[1] / H,
-        grad_spectral_in / H,
-        grad_spectral_out / H,
-        grad_spectral_bias / H,
+        grad_pin,
+        grad_pout,
+        grad_in,
+        grad_out,
+        grad_bias.reshape(2, NB, BS),
     )
 
 

time: 535 us -> 381 us (0.71)
  waiting for transfers between devices: 151 us -> 0 us
  Pallas kernels: 340 us -> 367 us
  between operations: 14.2 us -> 0.66 us
  other arithmetic: 12.7 us -> 1.65 us
    psum x1 -> x0, waiting for transfers between devices: 151 us -> none  [body(): early = lax.psum(jnp.stack([acc_in, acc_out]), ('row', 'col'))]
    pallas_call x1, Pallas kernels: 148 us -> 174 us  [backward_call(): pl.pallas_call(backward_kernel, out_shape=(shape((C, LR, LW), BF16), shap...]
    unnamed x18 -> x12, local copies, waits for them, and re-layouts: 11.6 us -> 10.6 us
  transfers between devices with their start and end apart: 1 -> 0, of which waited for: 1 -> 0; matrix products, arithmetic and copies ran while one was open for 0% -> 0% of each run, Pallas kernels for 0% -> 0%
where the time goes in v2:
time: 381 us
  Pallas kernels  367 us (96%)
  local copies, waits for them, and re-layouts  12.1 us (3%)
    pallas_call x1, Pallas kernels, backward_call(): pl.pallas_call(backward_kernel, out_shape=(shape((C, LR, LW), BF16), shap...  174 us
    pallas_call x1, Pallas kernels, forward_call(): pl.pallas_call(forward_kernel, out_shape=(shape((C, LR, LW), BF16), shape...  146 us
    pallas_call x1, Pallas kernels, token_call(): pl.pallas_call(token_kernel, grid=(LR // TR,), out_shape=(shape((C, LR, L...  46.8 us
    unnamed x12, local copies, waits for them, and re-layouts  10.6 us

profile of v2, /device:TPU:1, one launch (start us, length us, event | category | flops | bytes accessed | tf_op | source)
XLA Modules:
  0.0 381.1 jit_solution(3954389276835209400)
XLA Ops:
  0.6 1.5 copy.19.bias
  2.1 1.9 copy.20.pout
  4.0 145.5 %spectral_forward.1 = (bf16[192,64,128]{2,1,0:T(8,128)(2,1)}, bf16[192,64,128]{2,1,0:T(8,128)(2,1)}, bf16[192,2048]{1,0:T(8,128)(2,1)}, f32[192,2048]{1,0:T(8,12...) custom-call(bf16[192,64,128]{2,1,0:T(8,128)(2,1)} %weather.5, bf16[512,1024]{1,0:T(8,128)(2,1)} %constant.9.width, ...), custom_call_target="tpu_custom_call" | custom-call | tf_op jit(solution)/shard_map/spectral_forward/pallas_call | solution.py:708
  149.5 46.8 %token_block.1 = (bf16[192,64,128]{2,1,0:T(8,128)(2,1)}, f32[192,64,128]{2,1,0:T(8,128)}, f32[2,8,24,768]{3,2,1,0:T(8,128)}) custom-call(bf16[192,64,128]{2,1,0:T(8,128)(2,1)} %weather.5, bf16[192,64,128]{2,1,0:T(8,128)(2,1)} %get-tuple-element.22.normed_in, bf16[192,64,128]{2,1,0:T(8,128)(2,1)} %get-tuple-element.23.filtered, ...), custom_call_target="tpu_custom_call" | custom-call | tf_op jit(solution)/shard_map/token_block/pallas_call | solution.py:765
  196.4 174.4 %spectral_backward.1 = (bf16[192,64,128]{2,1,0:T(8,128)(2,1)}, f32[192,768]{1,0:T(8,128)}, f32[768,192]{1,0:T(8,128)}, f32[2,2,96,96]{3,2,1,0:T(8,128)}, f32[2,2...) custom-call(bf16[192,64,128]{2,1,0:T(8,128)(2,1)} %weather.5, f32[192,64,128]{2,1,0:T(8,128)} %get-tuple-element.25.grad_sum, ...), custom_call_target="tpu_custom_call" | custom-call | tf_op jit(solution)/shard_map/spectral_backward/pallas_call | solution.py:730
  370.7 1.7 reduce
  372.4 2.2 copy.21
  374.6 0.0 copy-start
  374.6 0.0 copy-start.2
  374.6 0.0 copy-start.1
  374.6 4.3 %copy.26 = bf16[192,64,128]{2,1,0:T(8,128)(2,1)} copy(bf16[192,64,128]{2,1,0:T(8,128)(2,1)} %get-tuple-element.59) | data formatting | bytes 6291456
  378.9 0.0 copy-done
  378.9 0.8 copy.27
  379.8 0.0 copy-done.2
  379.8 0.7 copy.28
  380.4 0.0 copy-done.1
  380.4 0.7 copy.29
Async XLA Ops:
  374.6 4.3 %copy-start = (f32[192,768]{1,0:T(8,128)S(1)}, f32[192,768]{1,0:T(8,128)}, u32[]{:S(2)}) copy-start(f32[192,768]{1,0:T(8,128)} %get-tuple-element.60) | copy-start | bytes 1769476
  374.6 5.1 %copy-start.2 = (f32[2,2,96,96]{3,2,1,0:T(8,128)S(1)}, f32[2,2,96,96]{3,2,1,0:T(8,128)}, u32[]{:S(2)}) copy-start(f32[2,2,96,96]{3,2,1,0:T(8,128)} %get-tuple-element.62) | copy-start | bytes 442372
  374.6 5.8 %copy-start.1 = (f32[2,2,96,96]{3,2,1,0:T(8,128)S(1)}, f32[2,2,96,96]{3,2,1,0:T(8,128)}, u32[]{:S(2)}) copy-start(f32[2,2,96,96]{3,2,1,0:T(8,128)} %get-tuple-element.63) | copy-start | bytes 442372

commit v3 on v2

--- a/solution.py
+++ b/solution.py
@@ -26,6 +26,10 @@
 NX = 4
 SG = 8
 MODES = 2048
+TR = 16
+RB = LR // TR
+TN = TR * LW
+CHUNK = 512
 EPS = 1e-05
 THRESHOLD = 0.1
 F32 = jnp.float32
@@ -72,9 +76,9 @@
 
 
 class Exchange:
-    def __init__(self, scratch):
-        (self.X, self.O, self.G, self.K, self.Y0, self.y32, self.Z0, self.Q, self.BK, self.F, self.FO) = scratch[:11]
-        self.sems = scratch[11:23]
+    def __init__(self, buffers, sems):
+        (self.X, self.O, self.G, self.K, self.Y0, self.y32, self.Z0, self.Q, self.BK, self.F, self.FO) = buffers
+        self.sems = sems
         self.ri = lax.axis_index("row")
         self.ci = lax.axis_index("col")
         self.core = self.ri % 2
@@ -118,6 +122,27 @@
             device_id_type=MESH,
         )
 
+    def rows1(self, src, r, d):
+        col, core = self.peer1(d)
+        rows = pl.ds(pl.multiple_of(r * TR, TR), TR)
+        there = pl.ds(pl.multiple_of(self.core * LR + r * TR, TR), TR)
+        return pltpu.make_async_remote_copy(
+            src_ref=src.at[pl.ds(self.first_channel(col, core), CG), rows, :],
+            dst_ref=self.X.at[self.ci, :, there, :],
+            send_sem=self.sems[0].at[r, d],
+            recv_sem=self.sems[1].at[r, d],
+            device_id=(2 * self.s + core, col),
+            device_id_type=MESH,
+        )
+
+    def send_rows1(self, src, r):
+        rows = pl.ds(pl.multiple_of(r * TR, TR), TR)
+        there = pl.ds(pl.multiple_of(self.core * LR + r * TR, TR), TR)
+        own = self.first_channel(self.ci, self.core)
+        for d in range(1, 16):
+            self.rows1(src, r, d).start()
+        self.X[self.ci, :, there, :] = src[pl.ds(own, CG), rows, :]
+
     def send1(self, src):
         rows = pl.ds(pl.multiple_of(self.core * LR, LR), LR)
         own = self.first_channel(self.ci, self.core)
@@ -137,11 +162,19 @@
             device_id_type=MESH,
         )
 
-    def width_forward(self, src, table):
+    def width_forward(self, src, table, by_rows):
+        if by_rows:
+
+            @pl.loop(0, RB)
+            def _(r):
+                for d in range(1, 16):
+                    self.rows1(src, r, d).wait_recv()
+
         @pl.loop(0, NCH)
         def _(i):
-            for d in range(1, 16):
-                self.copy1(src, i, d).wait_recv()
+            if not by_rows:
+                for d in range(1, 16):
+                    self.copy1(src, i, d).wait_recv()
             for half in range(CH // 2):
                 c = i * CH + 2 * half
                 field = jnp.concatenate(
@@ -201,13 +234,13 @@
                     pl.ds(part * 16 + k, BS, stride=32), :
                 ].astype(BF16)
 
-    def copyz(self, e):
+    def copyz(self, i, e):
         x, core = self.peer2(e)
         return pltpu.make_async_remote_copy(
-            src_ref=self.Z0.at[x * 2 + core],
-            dst_ref=self.Q.at[self.x, :, :, pl.ds(pl.multiple_of(self.core * 16, 16), 16), :],
-            send_sem=self.sems[6].at[e],
-            recv_sem=self.sems[7].at[e],
+            src_ref=self.Z0.at[x * 2 + core, pl.ds(i * CH, CH)],
+            dst_ref=self.Q.at[self.x, pl.ds(i * CH, CH), :, pl.ds(pl.multiple_of(self.core * 16, 16), 16), :],
+            send_sem=self.sems[6].at[i, e],
+            recv_sem=self.sems[7].at[i, e],
             device_id=(2 * self.s + core, 2 * x + self.yh),
             device_id_type=MESH,
         )
@@ -221,8 +254,9 @@
                         part * BS : (part + 1) * BS, j * 128 : (j + 1) * 128
                     ]
         self.Z0[...] = self.y32[...].astype(BF16).reshape(8, CG, 2, 16, 128)
-        for e in range(1, 8):
-            self.copyz(e).start()
+        for i in range(NCH):
+            for e in range(1, 8):
+                self.copyz(i, e).start()
         self.Q[self.x, :, :, pl.ds(pl.multiple_of(self.core * 16, 16), 16), :] = self.Z0[self.id2]
 
     def copyf(self, i, e):
@@ -237,11 +271,10 @@
         )
 
     def height_inverse(self, table):
-        for e in range(1, 8):
-            self.copyz(e).wait_recv()
-
         @pl.loop(0, NCH)
         def _(i):
+            for e in range(1, 8):
+                self.copyz(i, e).wait_recv()
             own = pl.ds(i * CH, CH)
             modes = jnp.concatenate([self.Q[x, own].reshape(CH * 64, 128) for x in range(NX)], axis=1)
             for q in range(4):
@@ -271,7 +304,20 @@
             device_id_type=MESH,
         )
 
-    def width_inverse(self, out, table):
+    def rowso(self, out, r, d):
+        col, core = self.peer1(d)
+        rows = pl.ds(pl.multiple_of(core * LR + r * TR, TR), TR)
+        there = pl.ds(pl.multiple_of(r * TR, TR), TR)
+        return pltpu.make_async_remote_copy(
+            src_ref=self.FO.at[col, :, rows, :],
+            dst_ref=out.at[pl.ds(self.first_channel(self.ci, self.core), CG), there, :],
+            send_sem=self.sems[10].at[r, d],
+            recv_sem=self.sems[11].at[r, d],
+            device_id=(2 * self.s + core, col),
+            device_id_type=MESH,
+        )
+
+    def width_inverse(self, out, table, by_rows):
         rows = pl.ds(pl.multiple_of(self.core * LR, LR), LR)
         start = self.first_channel(self.ci, self.core)
 
@@ -291,34 +337,40 @@
                         self.FO[2 * q + j, pl.ds(c, 2)] = field[:, j * 128 : (j + 1) * 128].reshape(
                             2, 128, 128
                         )
+            if not by_rows:
+                for d in range(1, 16):
+                    self.copyo(out, i, d).start()
+            out[pl.ds(start + i * CH, CH)] = self.FO[self.ci, pl.ds(i * CH, CH), rows, :]
+
+        if by_rows:
+
+            @pl.loop(0, RB)
+            def _(r):
+                for d in range(1, 16):
+                    self.rowso(out, r, d).start()
+
+    def drain(self, src, first):
+        @pl.loop(0, RB if first else NCH)
+        def _(i):
             for d in range(1, 16):
-                self.copyo(out, i, d).start()
-            out[pl.ds(start + i * CH, CH)] = self.FO[self.ci, pl.ds(i * CH, CH), rows, :]
-
-    def finish(self, src, out):
+                (self.rows1 if first else self.copy1)(src, i, d).wait_send()
+
         @pl.loop(0, NCH)
         def _(i):
-            for d in range(1, 16):
-                self.copyo(out, i, d).wait_recv()
-        self.drain(src, out)
-
-    def drain(self, src, out):
-        @pl.loop(0, NCH)
+            for e in range(1, 8):
+                self.copyb(i, e).wait_send()
+                self.copyc(i, e).wait_send()
+                self.copyz(i, e).wait_send()
+                self.copyf(i, e).wait_send()
+
+    def drain_out(self, out, by_rows):
+        @pl.loop(0, RB if by_rows else NCH)
         def _(i):
             for d in range(1, 16):
-                self.copy1(src, i, d).wait_send()
-                self.copyo(out, i, d).wait_send()
-            for e in range(1, 8):
-                self.copyb(i, e).wait_send()
-                self.copyc(i, e).wait_send()
-                self.copyf(i, e).wait_send()
-        for e in range(1, 8):
-            self.copyz(e).wait_send()
+                (self.rowso if by_rows else self.copyo)(out, i, d).wait_send()
 
 
 def exchange_scratch():
-    dma = pltpu.SemaphoreType.DMA
-    pairs = [(NCH, 16), (NCH, 8), (NCH, 8), (8,), (NCH, 8), (NCH, 16)]
     return [
         pltpu.VMEM((8, CG, 2 * LR, LW), BF16),
         pltpu.VMEM((SG, CG, 64, 128), BF16),
@@ -331,7 +383,13 @@
         pltpu.VMEM((SG, CG, 64, 128), BF16),
         pltpu.VMEM((SG, CG, 64, 128), BF16),
         pltpu.VMEM((8, CG, 2 * LR, LW), BF16),
-    ] + [dma(shape) for shape in pairs for _ in range(2)]
+    ]
+
+
+def exchange_semaphores():
+    most = max(NCH, RB)
+    pairs = [(most, 16), (NCH, 8), (NCH, 8), (NCH, 8), (NCH, 8), (most, 16)]
+    return [pltpu.SemaphoreType.DMA(shape) for shape in pairs for _ in range(2)]
 
 
 class Reduction:
@@ -433,12 +491,11 @@
                 self.copy_d(e).wait_send()
 
 
-def reduction_scratch(rows, lanes, source):
+def reduction_scratch(rows, lanes):
     dma = pltpu.SemaphoreType.DMA
     part = pltpu.VMEM((8, rows, lanes), F32)
-    buffers = [pltpu.VMEM((2, 8, rows, lanes), F32)] if source else []
     return (
-        buffers
+        [pltpu.VMEM((2, 8, rows, lanes), F32)]
         + [part, part, part, pltpu.VMEM((rows, lanes), F32), part, pltpu.VMEM((2, 8, rows, lanes), F32)]
         + [dma] * 2
         + [dma((8,))] * 6
@@ -453,51 +510,101 @@
     return total * (1.0 / C)
 
 
-def norm_rows(field, rows):
-    mean = channel_mean(lambda c: field[c, rows, :].astype(F32))
+def token_rows(r, weather, normed, filtered, cot, pin, pin_t, pout, pout_t, acc_in, acc_out,
+               s32, x32, gc, normal_low, cot_low, output, out_copy, sum_copy, next_cot):
+    rows = pl.ds(pl.multiple_of(r * TR, TR), TR)
+    g32, c32 = gc.at[0], gc.at[1]
+
+    def at(c):
+        return slice(c * TR, (c + 1) * TR)
+
+    total = jnp.zeros((TR, LW), F32)
+    for c in range(C):
+        value = (
+            weather[c, rows, :].astype(F32)
+            + normed[c, rows, :].astype(F32)
+            + filtered[c, rows, :].astype(F32)
+        )
+        s32[at(c), :] = value
+        total = total + value
+        c32[at(c), :] = cot[c].astype(F32)
+
+    @pl.when(r < RB - 1)
+    def _():
+        next_cot(r + 1).start()
+
+    mean = total * (1.0 / C)
 
     def square(c):
-        centred = field[c, rows, :].astype(F32) - mean
+        centred = s32[at(c), :] - mean
         return centred * centred
 
-    return mean, lax.rsqrt(channel_mean(square) + EPS)
-
-
-def forward_kernel(
-    weather, width, weighted, height, spectral_in, bias, spectral_out,
-    normed, filtered, kept, before_out, hidden_out, slope_out, *scratch
-):
-    ex = Exchange(scratch)
-
-    @pl.loop(0, LR // 16)
-    def _(r):
-        rows = pl.ds(pl.multiple_of(r * 16, 16), 16)
-        mean, spread = norm_rows(weather, rows)
-        for c in range(C):
-            normed[c, rows, :] = ((weather[c, rows, :].astype(F32) - mean) * spread).astype(BF16)
-
-    ex.barrier()
-    ex.send1(normed)
-    ex.width_forward(normed, width)
-    ex.height_forward(height)
-    ex.modes(kept)
-
+    spread = lax.rsqrt(channel_mean(square) + EPS)
+    for c in range(C):
+        x32[at(c), :] = (s32[at(c), :] - mean) * spread
+    for j in range(TR):
+        lanes = slice(j * LW, (j + 1) * LW)
+        normal_low[:, lanes] = x32[pl.ds(j, C, stride=TR), :].astype(BF16)
+        cot_low[:, lanes] = c32[pl.ds(j, C, stride=TR), :].astype(BF16)
+
+    @pl.when(r > 0)
+    def _():
+        sum_copy(r).wait()
+        out_copy(r).wait()
+
+    @pl.loop(0, TN // CHUNK)
+    def _(q):
+        lanes = pl.ds(pl.multiple_of(q * CHUNK, CHUNK), CHUNK)
+        normal = normal_low[:, lanes]
+        cot_now = cot_low[:, lanes]
+        before = dot_nn(pin_t[...], normal)
+        cumulative, density = normal_parts(before)
+        hidden = (before * cumulative).astype(BF16)
+        back_hidden = dot_nn(pout[...], cot_now)
+        back_before = (back_hidden * (cumulative + before * density)).astype(BF16)
+        out = dot_nn(pout_t[...], hidden)
+        back_normed = dot_nn(pin[...], back_before)
+        acc_out[...] += dot_nt(hidden, cot_now)
+        acc_in[...] += dot_nt(back_before, normal)
+        for j in range(CHUNK // LW):
+            sl = slice(j * LW, (j + 1) * LW)
+            where = pl.ds(q * (CHUNK // LW) + j, C, stride=TR)
+            s32[where, :] += out[:, sl]
+            g32[where, :] = back_normed[:, sl]
+
+    for c in range(C):
+        output[c] = s32[at(c), :].astype(BF16)
+    out_copy(r).start()
+    mean_grad = channel_mean(lambda c: g32[at(c), :])
+    mean_cross = channel_mean(lambda c: g32[at(c), :] * x32[at(c), :])
+    for c in range(C):
+        inner = g32[at(c), :] - mean_grad - x32[at(c), :] * mean_cross
+        value = c32[at(c), :] + spread * inner
+        g32[at(c), :] = value
+        normed[c, rows, :] = value.astype(BF16)
+    sum_copy(r).start()
+
+
+def mix_forward(ex, kept, before_all, hidden_all, slope_all, spectral_in, bias, spectral_out):
     a_re, a_im = spectral_in[0, ex.yh], spectral_in[1, ex.yh]
     b_re, b_im = spectral_out[0, ex.yh], spectral_out[1, ex.yh]
+    bias_re, bias_im = (
+        jnp.broadcast_to(bias[part, pl.ds(ex.yh, 1), :], (BS, BS)).T[:, :1] for part in range(2)
+    )
 
     def mixed(lo, hi):
         real, imaginary = kept[:BS, lo:hi], kept[BS:, lo:hi]
         before = jnp.concatenate(
             [
-                dot_tn(a_re, real) - dot_tn(a_im, imaginary) + bias[0, ex.yh],
-                dot_tn(a_re, imaginary) + dot_tn(a_im, real) + bias[1, ex.yh],
+                dot_tn(a_re, real) - dot_tn(a_im, imaginary) + bias_re,
+                dot_tn(a_re, imaginary) + dot_tn(a_im, real) + bias_im,
             ],
             axis=0,
         )
-        before_out[:, lo:hi] = before
+        before_all[:, lo:hi] = before
         cumulative, _ = normal_parts(before)
         hidden = (before * cumulative).astype(BF16)
-        hidden_out[:, lo:hi] = hidden
+        hidden_all[:, lo:hi] = hidden
         real, imaginary = hidden[:BS], hidden[BS:]
         second = jnp.concatenate(
             [
@@ -507,39 +614,13 @@
             axis=0,
         )
         slope = jnp.tanh(second * (1.0 / THRESHOLD))
-        slope_out[:, lo:hi] = slope
+        slope_all[:, lo:hi] = slope
         return second - THRESHOLD * slope
 
     ex.from_modes(mixed)
-    ex.height_inverse(height)
-    ex.width_inverse(filtered, weighted)
-    ex.finish(normed, filtered)
-
-
-def backward_kernel(
-    weather, grad_sum, token_grads, width, weighted, height, spectral_in, spectral_out,
-    kept, before, hidden, slope,
-    grad_weather, grad_pin, grad_pout, grad_in, grad_out, grad_bias,
-    low, filtered, grads, gate, *scratch
-):
-    ex = Exchange(scratch)
-    first = Reduction(ex, (token_grads,) + scratch[23:39])
-    other = Reduction(ex, scratch[39:56])
-
-    @pl.loop(0, LR // 16)
-    def _(r):
-        rows = pl.ds(pl.multiple_of(r * 16, 16), 16)
-        for c in range(C):
-            low[c, rows, :] = grad_sum[c, rows, :].astype(BF16)
-
-    ex.barrier()
-    first.round(0)
-    ex.send1(low)
-    ex.width_forward(low, weighted)
-    first.round(1)
-    ex.height_forward(height)
-    first.round(2)
-    ex.modes(grads)
+
+
+def mix_backward(ex, grads, gate, before, slope, spectral_in, spectral_out):
     a_re, a_im = spectral_in[0, ex.yh], spectral_in[1, ex.yh]
     b_re, b_im = spectral_out[0, ex.yh], spectral_out[1, ex.yh]
 
@@ -569,8 +650,9 @@
         )
 
     ex.from_modes(mixed)
-    first.round(3)
-    sums = other.src
+
+
+def spectral_sums(ex, sums, kept, gate, hidden, grads):
     sums[...] = jnp.zeros_like(sums)
     low_half, high_half = slice(0, BS), slice(BS, 2 * BS)
     for base, left, right in ((0, kept, gate), (2, hidden, grads)):
@@ -586,223 +668,223 @@
     for part in range(2):
         value = jnp.sum(gate[part * BS : (part + 1) * BS, :].astype(F32), axis=1, keepdims=True)
         sums[ex.yh, 2 * part : 2 * part + 2, :, BS : BS + 1] = value.reshape(2, 48, 1)
+
+
+def layer_kernel(
+    weather, cotangent, width, weighted, height, spectral_in, bias, spectral_out, pin, pout_t,
+    output, grad_weather, grad_pin, grad_pout_t, grad_in, grad_out, grad_bias, sum_hbm, *scratch
+):
+    (normed, filtered, stats, cot, out_block, kept, before, hidden, slope, grads, gate,
+     acc_in, acc_out, pin_t, pout, x32, gc, normal_low, cot_low, cot_sem, out_sem, sum_sem) = scratch[:22]
+    scratch = scratch[22:]
+    buffers, scratch = scratch[:11], scratch[11:]
+    ex = Exchange(buffers, scratch[:12])
+    back = Exchange(buffers, scratch[12:24])
+    first = Reduction(ex, scratch[24:41])
+    other = Reduction(ex, scratch[41:58])
+    s32 = ex.y32
+
+    def rows_of(r):
+        return pl.ds(pl.multiple_of(r * TR, TR), TR)
+
+    def next_cot(r):
+        return pltpu.make_async_copy(cotangent.at[:, rows_of(r), :], cot, cot_sem)
+
+    def out_copy(r):
+        return pltpu.make_async_copy(out_block, output.at[:, rows_of(r), :], out_sem)
+
+    def sum_copy(r):
+        return pltpu.make_async_copy(gc.at[0], sum_hbm.at[r], sum_sem)
+
+    def grad_copy(r):
+        return pltpu.make_async_copy(out_block, grad_weather.at[:, rows_of(r), :], out_sem)
+
+    next_cot(0).start()
+
+    @pl.loop(0, RB)
+    def _(r):
+        rows = rows_of(r)
+        mean = channel_mean(lambda c: weather[c, rows, :].astype(F32))
+
+        def square(c):
+            centred = weather[c, rows, :].astype(F32) - mean
+            return centred * centred
+
+        spread = lax.rsqrt(channel_mean(square) + EPS)
+        stats[0, rows, :] = mean
+        stats[1, rows, :] = spread
+        for c in range(C):
+            normed[c, rows, :] = ((weather[c, rows, :].astype(F32) - mean) * spread).astype(BF16)
+
+    ex.barrier()
+    ex.send1(normed)
+    pin_t[...] = pin[...].T
+    pout[...] = pout_t[...].T
+    acc_in[...] = jnp.zeros_like(acc_in)
+    acc_out[...] = jnp.zeros_like(acc_out)
+    ex.width_forward(normed, width, False)
+    ex.height_forward(height)
+    ex.modes(kept)
+    mix_forward(ex, kept, before, hidden, slope, spectral_in, bias, spectral_out)
+    ex.height_inverse(height)
+    ex.width_inverse(filtered, weighted, True)
+    ex.drain(normed, False)
+
+    @pl.loop(0, RB)
+    def _(r):
+        for d in range(1, 16):
+            ex.rowso(filtered, r, d).wait_recv()
+        next_cot(r).wait()
+        token_rows(
+            r, weather, normed, filtered, cot, pin, pin_t, pout, pout_t, acc_in, acc_out,
+            s32, x32, gc, normal_low, cot_low, out_block, out_copy, sum_copy, next_cot,
+        )
+        back.send_rows1(normed, r)
+
+    first.src[0] = acc_in[...].T.reshape(8, 24, HID)
+    first.src[1] = acc_out[...].T.reshape(8, 24, HID)
+    first.round(0)
+    sum_copy(0).wait()
+    out_copy(0).wait()
+    ex.drain_out(filtered, True)
+    back.width_forward(normed, weighted, True)
+    first.round(1)
+    back.height_forward(height)
+    first.round(2)
+    back.modes(grads)
+    mix_backward(back, grads, gate, before, slope, spectral_in, spectral_out)
+    first.round(3)
+    spectral_sums(back, other.src, kept, gate, hidden, grads)
     other.round(0)
-    ex.height_inverse(height)
+    back.height_inverse(height)
     first.round(4)
     other.round(1)
-    ex.width_inverse(filtered, width)
+    back.width_inverse(filtered, width, False)
     other.round(2)
     first.round(5)
     other.round(3)
     grad_pin[...] = first.out[0].reshape(C, HID)
-    grad_pout[...] = first.out[1].reshape(C, HID).T
+    grad_pout_t[...] = first.out[1].reshape(C, HID)
     other.round(4)
-    ex.finish(low, filtered)
+
+    def sum_back(r, slot):
+        return pltpu.make_async_copy(sum_hbm.at[r], gc.at[slot], sum_sem)
+
+    sum_back(0, 0).start()
+
+    @pl.loop(0, NCH)
+    def _(i):
+        for d in range(1, 16):
+            back.copyo(filtered, i, d).wait_recv()
+
+    @pl.loop(0, RB)
+    def _(r):
+        rows = rows_of(r)
+        slot = r % 2
+        sum_back(r, slot).wait()
+
+        @pl.when(r < RB - 1)
+        def _():
+            sum_back(r + 1, 1 - slot).start()
+
+        mean = stats[0, rows, :]
+        spread = stats[1, rows, :]
+
+        def own(c):
+            return gc[slot, pl.ds(c * TR, TR), :]
+
+        def total(c):
+            return own(c) + filtered[c, rows, :].astype(F32)
+
+        def normal(c):
+            return (weather[c, rows, :].astype(F32) - mean) * spread
+
+        mean_grad = channel_mean(total)
+        mean_cross = channel_mean(lambda c: total(c) * normal(c))
+
+        @pl.when(r > 0)
+        def _():
+            grad_copy(r).wait()
+
+        for c in range(C):
+            inner = total(c) - mean_grad - normal(c) * mean_cross
+            out_block[c] = (own(c) + spread * inner).astype(BF16)
+        grad_copy(r).start()
+
     other.round(5)
     for block in range(2):
         for part in range(2):
             for base, target in ((0, grad_in), (2, grad_out)):
                 at = 2 * (base + part)
                 target[part, block] = other.out[block, at : at + 2, :, :BS].reshape(BS, BS)
-            grad_bias[part, block] = other.out[block, 2 * part : 2 * part + 2, :, BS : BS + 1].reshape(BS, 1)
-
-    @pl.loop(0, LR // 16)
-    def _(r):
-        rows = pl.ds(pl.multiple_of(r * 16, 16), 16)
-        mean, spread = norm_rows(weather, rows)
-
-        def total(c):
-            return grad_sum[c, rows, :] + filtered[c, rows, :].astype(F32)
-
-        def normal(c):
-            return (weather[c, rows, :].astype(F32) - mean) * spread
-
-        mean_grad = channel_mean(total)
-        mean_cross = channel_mean(lambda c: total(c) * normal(c))
-        for c in range(C):
-            inner = total(c) - mean_grad - normal(c) * mean_cross
-            grad_weather[c, rows, :] = (grad_sum[c, rows, :] + spread * inner).astype(BF16)
-
-
-TR = 16
-TN = TR * LW
-CHUNK = 512
-
-
-def token_kernel(
-    weather, normed_in, filtered, cotangent, pin, pout,
-    output, grad_sum, grads, acc_in, acc_out, pin_t, pout_t, s32, x32, c32, g32, normal_low, cot_low
-):
-    step = pl.program_id(0)
-
-    @pl.when(step == 0)
-    def _():
-        acc_in[...] = jnp.zeros_like(acc_in)
-        acc_out[...] = jnp.zeros_like(acc_out)
-        pin_t[...] = pin[...].T
-        pout_t[...] = pout[...].T
-
-    def at(c):
-        return slice(c * TR, (c + 1) * TR)
-
-    total = jnp.zeros((TR, LW), F32)
-    for c in range(C):
-        value = weather[c].astype(F32) + normed_in[c].astype(F32) + filtered[c].astype(F32)
-        s32[at(c), :] = value
-        total = total + value
-        c32[at(c), :] = cotangent[c].astype(F32)
-    mean = total * (1.0 / C)
-
-    def square(c):
-        centred = s32[at(c), :] - mean
-        return centred * centred
-
-    spread = lax.rsqrt(channel_mean(square) + EPS)
-    for c in range(C):
-        x32[at(c), :] = (s32[at(c), :] - mean) * spread
-    for j in range(TR):
-        lanes = slice(j * LW, (j + 1) * LW)
-        normal_low[:, lanes] = x32[pl.ds(j, C, stride=TR), :].astype(BF16)
-        cot_low[:, lanes] = c32[pl.ds(j, C, stride=TR), :].astype(BF16)
-
-    @pl.loop(0, TN // CHUNK)
-    def _(q):
-        lanes = pl.ds(pl.multiple_of(q * CHUNK, CHUNK), CHUNK)
-        normal = normal_low[:, lanes]
-        cot = cot_low[:, lanes]
-        before = dot_nn(pin_t[...], normal)
-        cumulative, density = normal_parts(before)
-        hidden = (before * cumulative).astype(BF16)
-        back_hidden = dot_nn(pout[...], cot)
-        back_before = (back_hidden * (cumulative + before * density)).astype(BF16)
-        out = dot_nn(pout_t[...], hidden)
-        back_normed = dot_nn(pin[...], back_before)
-        acc_out[...] += dot_nt(hidden, cot)
-        acc_in[...] += dot_nt(back_before, normal)
-        for j in range(CHUNK // LW):
-            sl = slice(j * LW, (j + 1) * LW)
-            where = pl.ds(q * (CHUNK // LW) + j, C, stride=TR)
-            s32[where, :] += out[:, sl]
-            g32[where, :] = back_normed[:, sl]
-
-    for c in range(C):
-        output[c] = s32[at(c), :].astype(BF16)
-    mean_grad = channel_mean(lambda c: g32[at(c), :])
-    mean_cross = channel_mean(lambda c: g32[at(c), :] * x32[at(c), :])
-    for c in range(C):
-        inner = g32[at(c), :] - mean_grad - x32[at(c), :] * mean_cross
-        grad_sum[c] = c32[at(c), :] + spread * inner
-
-    @pl.when(step == pl.num_programs(0) - 1)
-    def _():
-        grads[0] = acc_in[...].T.reshape(8, 24, HID)
-        grads[1] = acc_out[...].T.reshape(8, 24, HID)
-
-
-def vmem():
-    return pl.BlockSpec(memory_space=pltpu.VMEM)
-
-
-def forward_call(*args):
+            column = other.out[block, 2 * part : 2 * part + 2, :, BS : BS + 1].reshape(BS, 1)
+            grad_bias[part, block : block + 1, :] = jnp.broadcast_to(column, (BS, BS)).T[:1, :]
+    back.drain(normed, True)
+    back.drain_out(filtered, False)
+    grad_copy(0).wait()
+
+
+def layer_call(*args):
     shape = jax.ShapeDtypeStruct
+    dma = pltpu.SemaphoreType.DMA
+    vmem, anywhere = (pl.BlockSpec(memory_space=space) for space in (pltpu.VMEM, pl.ANY))
     return pl.pallas_call(
-        forward_kernel,
+        layer_kernel,
         out_shape=(
             shape((C, LR, LW), BF16),
             shape((C, LR, LW), BF16),
-            shape((C, MODES), BF16),
-            shape((C, MODES), F32),
-            shape((C, MODES), BF16),
-            shape((C, MODES), F32),
-        ),
-        in_specs=[vmem()] * 7,
-        out_specs=[vmem()] * 6,
-        scratch_shapes=exchange_scratch(),
-        compiler_params=pltpu.CompilerParams(
-            collective_id=0, has_side_effects=True, vmem_limit_bytes=60 << 20
-        ),
-        name="spectral_forward",
-    )(*args)
-
-
-def backward_call(*args):
-    shape = jax.ShapeDtypeStruct
-    return pl.pallas_call(
-        backward_kernel,
-        out_shape=(
-            shape((C, LR, LW), BF16),
             shape((C, HID), F32),
-            shape((HID, C), F32),
+            shape((C, HID), F32),
             shape((2, NB, BS, BS), F32),
             shape((2, NB, BS, BS), F32),
-            shape((2, NB, BS, 1), F32),
+            shape((2, NB, BS), F32),
+            shape((RB, C * TR, LW), F32),
         ),
-        in_specs=[vmem()] * 12,
-        out_specs=[vmem()] * 6,
+        in_specs=[vmem, anywhere] + [vmem] * 8,
+        out_specs=[anywhere, anywhere] + [vmem] * 5 + [anywhere],
         scratch_shapes=[
             pltpu.VMEM((C, LR, LW), BF16),
             pltpu.VMEM((C, LR, LW), BF16),
+            pltpu.VMEM((2, LR, LW), F32),
+            pltpu.VMEM((C, TR, LW), BF16),
+            pltpu.VMEM((C, TR, LW), BF16),
+            pltpu.VMEM((C, MODES), BF16),
+            pltpu.VMEM((C, MODES), F32),
+            pltpu.VMEM((C, MODES), BF16),
+            pltpu.VMEM((C, MODES), F32),
             pltpu.VMEM((C, MODES), BF16),
             pltpu.VMEM((C, MODES), BF16),
+            pltpu.VMEM((HID, C), F32),
+            pltpu.VMEM((HID, C), F32),
+            pltpu.VMEM((HID, C), BF16),
+            pltpu.VMEM((HID, C), BF16),
+            pltpu.VMEM((C * TR, LW), F32),
+            pltpu.VMEM((2, C * TR, LW), F32),
+            pltpu.VMEM((C, TN), BF16),
+            pltpu.VMEM((C, TN), BF16),
+            dma,
+            dma,
+            dma,
         ]
         + exchange_scratch()
-        + reduction_scratch(24, HID, False)
-        + reduction_scratch(48, 128, True),
+        + exchange_semaphores()
+        + exchange_semaphores()
+        + reduction_scratch(24, HID)
+        + reduction_scratch(48, 128),
         compiler_params=pltpu.CompilerParams(
-            collective_id=1, has_side_effects=True, vmem_limit_bytes=63 << 20
+            collective_id=0, has_side_effects=True, vmem_limit_bytes=67043328
         ),
-        name="spectral_backward",
-    )(*args)
-
-
-def token_call(*args):
-    shape = jax.ShapeDtypeStruct
-    block = pl.BlockSpec((C, TR, LW), lambda i: (0, i, 0))
-
-    def whole(*dims):
-        return pl.BlockSpec(dims, lambda i: (0,) * len(dims))
-
-    return pl.pallas_call(
-        token_kernel,
-        grid=(LR // TR,),
-        out_shape=(
-            shape((C, LR, LW), BF16),
-            shape((C, LR, LW), F32),
-            shape((2, 8, 24, HID), F32),
-        ),
-        in_specs=[block] * 4 + [whole(C, HID), whole(HID, C)],
-        out_specs=[block, block, whole(2, 8, 24, HID)],
-        scratch_shapes=[pltpu.VMEM((HID, C), F32)] * 2
-        + [pltpu.VMEM((HID, C), BF16), pltpu.VMEM((C, HID), BF16)]
-        + [pltpu.VMEM((C * TR, LW), F32)] * 4
-        + [pltpu.VMEM((C, TN), BF16)] * 2,
-        compiler_params=pltpu.CompilerParams(vmem_limit_bytes=60 << 20),
-        name="token_block",
+        name="layer",
     )(*args)
 
 
 def body(weather, cotangent, spectral_in, spectral_bias, spectral_out, project_in, project_out):
     width, weighted, height = tables()
-    bias = spectral_bias.reshape(2, NB, BS, 1)
-    normed, filtered, kept, before, hidden, slope = forward_call(
-        weather, width, weighted, height, spectral_in, bias, spectral_out
+    output, grad_weather, grad_pin, grad_pout_t, grad_in, grad_out, grad_bias, _ = layer_call(
+        weather, cotangent, width, weighted, height, spectral_in, spectral_bias, spectral_out,
+        project_in, project_out.T,
     )
-    output, grad_sum, token_grads = token_call(
-        weather, normed, filtered, cotangent, project_in, project_out
-    )
-    grad_weather, grad_pin, grad_pout, grad_in, grad_out, grad_bias = backward_call(
-        weather, grad_sum, token_grads, width, weighted, height, spectral_in, spectral_out,
-        kept, before, hidden, slope,
-    )
-    return (
-        output,
-        grad_weather,
-        grad_pin,
-        grad_pout,
-        grad_in,
-        grad_out,
-        grad_bias.reshape(2, NB, BS),
-    )
+    return output, grad_weather, grad_pin, grad_pout_t.T, grad_in, grad_out, grad_bias
 
 
 def solution(mesh):

time: 381 us -> 322 us (0.85); the launches traced: 381 us -> 318 us
  Pallas kernels: 367 us -> 307 us
    pallas_call x3 -> x1, Pallas kernels: 367 us -> 307 us  [layer_call(): pl.pallas_call(layer_kernel, out_shape=(shape((C, LR, LW), BF16), shape((...]
    unnamed x12 -> x19, local copies, waits for them, and re-layouts: 10.6 us -> 9.65 us
where the time goes in v3:
time: 322 us; the launch traced here: 318 us
  Pallas kernels  307 us (95%)
  local copies, waits for them, and re-layouts  9.65 us (3%)
    pallas_call x1, Pallas kernels, layer_call(): pl.pallas_call(layer_kernel, out_shape=(shape((C, LR, LW), BF16), shape((...  307 us
    unnamed x19, local copies, waits for them, and re-layouts  9.65 us

profile of v3, /device:TPU:1, one launch (start us, length us, event | category | flops | bytes accessed | tf_op | source)
XLA Modules:
  0.0 317.7 jit_solution(3287334612234793279)
XLA Ops:
  0.6 307.4 %layer.1 = (bf16[192,64,128]{2,1,0:T(8,128)(2,1)}, bf16[192,64,128]{2,1,0:T(8,128)(2,1)}, f32[192,768]{1,0:T(8,128)}, f32[192,768]{1,0:T(8,128)}, f32[2,2,96,96]...) custom-call(bf16[192,64,128]{2,1,0:T(8,128)(2,1)} %weather.1, ...), custom_call_target="tpu_custom_call" | custom-call | tf_op jit(solution)/shard_map/layer/pallas_call | solution.py:831
  308.0 0.0 copy-start
  308.0 4.4 %copy.24 = bf16[192,64,128]{2,1,0:T(8,128)(2,1)} copy(bf16[192,64,128]{2,1,0:T(8,128)(2,1)} %get-tuple-element.28) | data formatting | bytes 6291456
  312.4 0.0 copy-done
  312.4 0.0 copy-start.2
  312.4 0.0 copy-start.1
  312.4 0.0 copy-start.4
  312.4 0.0 copy-start.3
  312.5 1.7 copy.25
  314.1 0.0 copy-done.2
  314.1 0.0 copy-start.5
  314.1 0.8 copy.26
  314.9 0.0 copy-done.1
  314.9 0.8 copy.27
  315.8 0.0 copy-done.4
  315.8 0.7 copy.28
  316.4 0.0 copy-done.3
  316.4 0.7 copy.29
  317.1 0.0 copy-done.5
  317.1 0.6 copy.30
Async XLA Ops:
  308.0 4.4 %copy-start = (bf16[192,64,128]{2,1,0:T(8,128)(2,1)S(1)}, bf16[192,64,128]{2,1,0:T(8,128)(2,1)}, u32[]{:S(2)}) copy-start(bf16[192,64,128]{2,1,0:T(8,128)(2,1)} %get-tuple-element.29) | copy-start | bytes 9437188
  312.4 1.7 copy-start.2
  312.4 2.5 copy-start.1
  312.4 3.3 %copy-start.4 = (f32[2,2,96,96]{3,2,1,0:T(8,128)S(1)}, f32[2,2,96,96]{3,2,1,0:T(8,128)}, u32[]{:S(2)}) copy-start(f32[2,2,96,96]{3,2,1,0:T(8,128)} %get-tuple-element.32) | copy-start | bytes 442372
  312.4 4.0 %copy-start.3 = (f32[2,2,96,96]{3,2,1,0:T(8,128)S(1)}, f32[2,2,96,96]{3,2,1,0:T(8,128)}, u32[]{:S(2)}) copy-start(f32[2,2,96,96]{3,2,1,0:T(8,128)} %get-tuple-element.33) | copy-start | bytes 442372
  314.1 3.0 copy-start.5

commit v4 on v3

--- a/solution.py
+++ b/solution.py
@@ -21,7 +21,7 @@
 LR = 64
 LW = 128
 CG = 12
-CH = 4
+CH = 2
 NCH = CG // CH
 NX = 4
 SG = 8
@@ -87,6 +87,8 @@
         self.yh = self.ci % 2
         self.id1 = self.ci * 2 + self.core
         self.id2 = self.x * 2 + self.core
+        self.z = self.s % 4
+        self.id3 = (self.s // 4) * 8 + self.ci
 
     def peer1(self, d):
         other = (self.id1 + d) % 16
@@ -96,7 +98,11 @@
         other = (self.id2 + e) % 8
         return other // 2, other % 2
 
-    def barrier(self):
+    def peer3(self, d):
+        other = (self.id3 + d) % 16
+        return other // 8, other % 8
+
+    def greet(self):
         sem = pltpu.get_barrier_semaphore()
         for d in range(1, 16):
             col, core = self.peer1(d)
@@ -104,7 +110,13 @@
         for e in range(1, SG):
             s = (self.s + e) % SG
             pl.semaphore_signal(sem, inc=1, device_id=(2 * s + self.core, self.ci), device_id_type=MESH)
-        pl.semaphore_wait(sem, 15 + SG - 1)
+        other_lo = 1 - self.s // 4
+        for e in range(1, 8):
+            row = 2 * (4 * other_lo + self.z) + self.core
+            pl.semaphore_signal(sem, inc=1, device_id=(row, (self.ci + e) % 8), device_id_type=MESH)
+
+    def barrier(self):
+        pl.semaphore_wait(pltpu.get_barrier_semaphore(), 15 + SG - 1 + 7)
 
     def first_channel(self, col, core):
         return (col % 2) * BS + (col // 2) * (2 * CG) + core * CG
@@ -393,112 +405,145 @@
 
 
 class Reduction:
-    def __init__(self, ex, scratch):
+    def __init__(self, ex, scratch, n):
         self.ex = ex
+        self.n = n
         self.src, self.ra, self.t1, self.rb, self.t2, self.rc, self.out = scratch[:7]
-        self.sems = scratch[7:17]
-
-    def copy_a(self):
+        self.sems = scratch[7:19]
+
+    def copy_a(self, dst, src, k):
         ex = self.ex
         return pltpu.make_async_remote_copy(
-            src_ref=self.src.at[1 - ex.core],
-            dst_ref=self.ra,
-            send_sem=self.sems[0],
-            recv_sem=self.sems[1],
+            src_ref=src,
+            dst_ref=dst,
+            send_sem=self.sems[k],
+            recv_sem=self.sems[k + 1],
             device_id=(2 * ex.s + 1 - ex.core, ex.ci),
             device_id_type=MESH,
         )
 
-    def copy_b(self, e):
+    def first_core(self):
+        return self.copy_a(self.ra, self.src.at[1 - self.ex.core], 0)
+
+    def last_core(self):
+        own = self.out.at[self.ex.core]
+        return self.copy_a(own, own, 10)
+
+    def over_z(self, dst, src, k, e):
         ex = self.ex
-        s = (ex.s + e) % SG
-        return pltpu.make_async_remote_copy(
-            src_ref=self.t1.at[s],
-            dst_ref=self.rb.at[ex.s],
-            send_sem=self.sems[2].at[e],
-            recv_sem=self.sems[3].at[e],
-            device_id=(2 * s + ex.core, ex.ci),
-            device_id_type=MESH,
-        )
-
-    def copy_c(self, e):
+        return pltpu.make_async_remote_copy(
+            src_ref=src,
+            dst_ref=dst,
+            send_sem=self.sems[k].at[e],
+            recv_sem=self.sems[k + 1].at[e],
+            device_id=(2 * ((ex.s // 4) * 4 + (ex.z + e) % 4) + ex.core, ex.ci),
+            device_id_type=MESH,
+        )
+
+    def first_z(self, e):
+        return self.over_z(self.rb.at[self.ex.z], self.t1.at[(self.ex.z + e) % 4], 2, e)
+
+    def last_z(self, e):
+        own = self.out.at[self.ex.core, self.ex.z]
+        return self.over_z(own, own, 8, e)
+
+    def over_rest(self, dst, src, k, d):
         ex = self.ex
-        return pltpu.make_async_remote_copy(
-            src_ref=self.t2,
-            dst_ref=self.rc.at[ex.ci],
-            send_sem=self.sems[4].at[e],
-            recv_sem=self.sems[5].at[e],
-            device_id=(ex.ri, (ex.ci + e) % 8),
-            device_id_type=MESH,
-        )
-
-    def copy_d(self, e):
-        ex = self.ex
-        return pltpu.make_async_remote_copy(
-            src_ref=self.out.at[ex.core, ex.s],
-            dst_ref=self.out.at[ex.core, ex.s],
-            send_sem=self.sems[6].at[e],
-            recv_sem=self.sems[7].at[e],
-            device_id=(2 * ((ex.s + e) % SG) + ex.core, ex.ci),
-            device_id_type=MESH,
-        )
-
-    def copy_e(self):
-        ex = self.ex
-        return pltpu.make_async_remote_copy(
-            src_ref=self.out.at[ex.core],
-            dst_ref=self.out.at[ex.core],
-            send_sem=self.sems[8],
-            recv_sem=self.sems[9],
-            device_id=(2 * ex.s + 1 - ex.core, ex.ci),
-            device_id_type=MESH,
-        )
+        low, col = ex.peer3(d)
+        return pltpu.make_async_remote_copy(
+            src_ref=src,
+            dst_ref=dst,
+            send_sem=self.sems[k].at[d],
+            recv_sem=self.sems[k + 1].at[d],
+            device_id=(2 * (low * 4 + ex.z) + ex.core, col),
+            device_id_type=MESH,
+        )
+
+    def guard(self, member, action):
+        pl.when(member < self.n)(action)
+
+    def peer(self, d):
+        return (self.ex.id3 + d) % 16
+
+    def piece_at(self, member):
+        return lax.min(member, self.n - 1)
+
+    def first_rest(self, d):
+        return self.over_rest(self.rc.at[self.ex.id3], self.t2.at[self.piece_at(self.peer(d))], 4, d)
+
+    def last_rest(self, d, member):
+        own = self.out.at[self.ex.core, self.ex.z, self.piece_at(member)]
+        return self.over_rest(own, own, 6, d)
 
     def round(self, number):
         ex = self.ex
         if number == 0:
-            self.copy_a().start()
+            self.first_core().start()
         elif number == 1:
-            self.copy_a().wait_recv()
+            self.first_core().wait_recv()
             self.t1[...] = self.src[ex.core] + self.ra[...]
-            for e in range(1, 8):
-                self.copy_b(e).start()
-            self.rb[ex.s] = self.t1[ex.s]
+            for e in range(1, 4):
+                self.first_z(e).start()
+            self.rb[ex.z] = self.t1[ex.z]
         elif number == 2:
-            for e in range(1, 8):
-                self.copy_b(e).wait_recv()
-            self.t2[...] = jnp.sum(self.rb[...], axis=0)
-            for e in range(1, 8):
-                self.copy_c(e).start()
-            self.rc[ex.ci] = self.t2[...]
+            for e in range(1, 4):
+                self.first_z(e).wait_recv()
+            self.t2[...] = self.rb[0] + self.rb[1] + self.rb[2] + self.rb[3]
+            for d in range(1, 16):
+                self.guard(self.peer(d), lambda d=d: self.first_rest(d).start())
+            self.guard(ex.id3, self.keep)
         elif number == 3:
-            for e in range(1, 8):
-                self.copy_c(e).wait_recv()
-            self.out[ex.core, ex.s] = jnp.sum(self.rc[...], axis=0) * (1.0 / H)
-            for e in range(1, 8):
-                self.copy_d(e).start()
+            self.guard(ex.id3, self.add)
         elif number == 4:
-            for e in range(1, 8):
-                self.copy_d(e).wait_recv()
-            self.copy_e().start()
+            for d in range(1, 16):
+                source = (ex.id3 + 16 - d) % 16
+                self.guard(source, lambda d=d, source=source: self.last_rest(d, source).wait_recv())
+            for e in range(1, 4):
+                self.last_z(e).start()
+        elif number == 5:
+            for e in range(1, 4):
+                self.last_z(e).wait_recv()
+            self.last_core().start()
         else:
-            self.copy_e().wait_recv()
-            self.copy_a().wait_send()
-            self.copy_e().wait_send()
-            for e in range(1, 8):
-                self.copy_b(e).wait_send()
-                self.copy_c(e).wait_send()
-                self.copy_d(e).wait_send()
-
-
-def reduction_scratch(rows, lanes):
+            self.last_core().wait_recv()
+            self.first_core().wait_send()
+            self.last_core().wait_send()
+            for e in range(1, 4):
+                self.first_z(e).wait_send()
+                self.last_z(e).wait_send()
+            for d in range(1, 16):
+                self.guard(self.peer(d), lambda d=d: self.first_rest(d).wait_send())
+            self.guard(ex.id3, self.sent)
+
+    def keep(self):
+        self.rc[self.ex.id3] = self.t2[self.piece_at(self.ex.id3)]
+
+    def add(self):
+        ex = self.ex
+        for d in range(1, 16):
+            self.first_rest(d).wait_recv()
+        total = self.rc[0]
+        for member in range(1, 16):
+            total = total + self.rc[member]
+        self.out[ex.core, ex.z, self.piece_at(ex.id3)] = total * (1.0 / H)
+        for d in range(1, 16):
+            self.last_rest(d, ex.id3).start()
+
+    def sent(self):
+        for d in range(1, 16):
+            self.last_rest(d, self.ex.id3).wait_send()
+
+
+def reduction_scratch(n):
     dma = pltpu.SemaphoreType.DMA
-    part = pltpu.VMEM((8, rows, lanes), F32)
+    part = pltpu.VMEM((4, n, 24, 128), F32)
+    whole = pltpu.VMEM((2, 4, n, 24, 128), F32)
     return (
-        [pltpu.VMEM((2, 8, rows, lanes), F32)]
-        + [part, part, part, pltpu.VMEM((rows, lanes), F32), part, pltpu.VMEM((2, 8, rows, lanes), F32)]
+        [whole, part, part, part, pltpu.VMEM((n, 24, 128), F32), pltpu.VMEM((16, 24, 128), F32), whole]
         + [dma] * 2
-        + [dma((8,))] * 6
+        + [dma((4,))] * 2
+        + [dma((16,))] * 4
+        + [dma((4,))] * 2
         + [dma] * 2
     )
 
@@ -663,25 +708,26 @@
             left[high_half, :], right[low_half, :]
         )
         for part, value in enumerate((real, imaginary)):
-            at = 2 * (base + part)
-            sums[ex.yh, at : at + 2, :, :BS] = value.reshape(2, 48, BS)
+            sums[ex.yh, base + part, :, :, :BS] = value.reshape(4, 24, BS)
     for part in range(2):
         value = jnp.sum(gate[part * BS : (part + 1) * BS, :].astype(F32), axis=1, keepdims=True)
-        sums[ex.yh, 2 * part : 2 * part + 2, :, BS : BS + 1] = value.reshape(2, 48, 1)
+        sums[ex.yh, part, :, :, BS : BS + 1] = value.reshape(4, 24, 1)
 
 
 def layer_kernel(
-    weather, cotangent, width, weighted, height, spectral_in, bias, spectral_out, pin, pout_t,
+    weather, cotangent, width_hbm, weighted_hbm, height_hbm, spectral_in, bias, spectral_out, pin, pout_t,
     output, grad_weather, grad_pin, grad_pout_t, grad_in, grad_out, grad_bias, sum_hbm, *scratch
 ):
     (normed, filtered, stats, cot, out_block, kept, before, hidden, slope, grads, gate,
-     acc_in, acc_out, pin_t, pout, x32, gc, normal_low, cot_low, cot_sem, out_sem, sum_sem) = scratch[:22]
-    scratch = scratch[22:]
+     acc_in, acc_out, pin_t, pout, x32, gc, normal_low, cot_low, width, weighted, height,
+     cot_sem, out_sem, sum_sem) = scratch[:25]
+    scratch = scratch[25:]
     buffers, scratch = scratch[:11], scratch[11:]
     ex = Exchange(buffers, scratch[:12])
     back = Exchange(buffers, scratch[12:24])
-    first = Reduction(ex, scratch[24:41])
-    other = Reduction(ex, scratch[41:58])
+    first = Reduction(ex, scratch[24:43], 12)
+    other = Reduction(ex, scratch[43:62], 4)
+    tables_sem = scratch[62]
     s32 = ex.y32
 
     def rows_of(r):
@@ -699,6 +745,13 @@
     def grad_copy(r):
         return pltpu.make_async_copy(out_block, grad_weather.at[:, rows_of(r), :], out_sem)
 
+    def fetch(at):
+        pairs = ((width_hbm, width), (height_hbm, height), (weighted_hbm, weighted))
+        return pltpu.make_async_copy(*pairs[at], tables_sem.at[at])
+
+    ex.greet()
+    for at in range(3):
+        fetch(at).start()
     next_cot(0).start()
 
     @pl.loop(0, RB)
@@ -722,6 +775,8 @@
     pout[...] = pout_t[...].T
     acc_in[...] = jnp.zeros_like(acc_in)
     acc_out[...] = jnp.zeros_like(acc_out)
+    for at in range(3):
+        fetch(at).wait()
     ex.width_forward(normed, width, False)
     ex.height_forward(height)
     ex.modes(kept)
@@ -741,36 +796,41 @@
         )
         back.send_rows1(normed, r)
 
-    first.src[0] = acc_in[...].T.reshape(8, 24, HID)
-    first.src[1] = acc_out[...].T.reshape(8, 24, HID)
+    for half, total in enumerate((acc_in, acc_out)):
+        turned = total[...].T
+        pieces = jnp.concatenate([turned[:, j * 128 : (j + 1) * 128] for j in range(HID // 128)], axis=0)
+        first.src[half] = pieces.reshape(4, 12, 24, 128)
     first.round(0)
     sum_copy(0).wait()
     out_copy(0).wait()
     ex.drain_out(filtered, True)
+    first.round(1)
     back.width_forward(normed, weighted, True)
-    first.round(1)
+    first.round(2)
     back.height_forward(height)
-    first.round(2)
+    first.round(3)
     back.modes(grads)
     mix_backward(back, grads, gate, before, slope, spectral_in, spectral_out)
-    first.round(3)
+    first.round(4)
     spectral_sums(back, other.src, kept, gate, hidden, grads)
     other.round(0)
+    first.round(5)
+    other.round(1)
     back.height_inverse(height)
-    first.round(4)
-    other.round(1)
+    other.round(2)
+    first.round(6)
+    for half, target in enumerate((grad_pin, grad_pout_t)):
+        pieces = first.out[half].reshape(HID // 128, C, 128)
+        for j in range(HID // 128):
+            target[:, j * 128 : (j + 1) * 128] = pieces[j]
     back.width_inverse(filtered, width, False)
-    other.round(2)
-    first.round(5)
     other.round(3)
-    grad_pin[...] = first.out[0].reshape(C, HID)
-    grad_pout_t[...] = first.out[1].reshape(C, HID)
-    other.round(4)
 
     def sum_back(r, slot):
         return pltpu.make_async_copy(sum_hbm.at[r], gc.at[slot], sum_sem)
 
     sum_back(0, 0).start()
+    other.round(4)
 
     @pl.loop(0, NCH)
     def _(i):
@@ -812,12 +872,12 @@
         grad_copy(r).start()
 
     other.round(5)
+    other.round(6)
     for block in range(2):
         for part in range(2):
             for base, target in ((0, grad_in), (2, grad_out)):
-                at = 2 * (base + part)
-                target[part, block] = other.out[block, at : at + 2, :, :BS].reshape(BS, BS)
-            column = other.out[block, 2 * part : 2 * part + 2, :, BS : BS + 1].reshape(BS, 1)
+                target[part, block] = other.out[block, base + part, :, :, :BS].reshape(BS, BS)
+            column = other.out[block, part, :, :, BS : BS + 1].reshape(BS, 1)
             grad_bias[part, block : block + 1, :] = jnp.broadcast_to(column, (BS, BS)).T[:1, :]
     back.drain(normed, True)
     back.drain_out(filtered, False)
@@ -840,7 +900,7 @@
             shape((2, NB, BS), F32),
             shape((RB, C * TR, LW), F32),
         ),
-        in_specs=[vmem, anywhere] + [vmem] * 8,
+        in_specs=[vmem] + [anywhere] * 4 + [vmem] * 5,
         out_specs=[anywhere, anywhere] + [vmem] * 5 + [anywhere],
         scratch_shapes=[
             pltpu.VMEM((C, LR, LW), BF16),
@@ -862,6 +922,9 @@
             pltpu.VMEM((2, C * TR, LW), F32),
             pltpu.VMEM((C, TN), BF16),
             pltpu.VMEM((C, TN), BF16),
+            pltpu.VMEM((2 * KW, W), BF16),
+            pltpu.VMEM((2 * KW, W), BF16),
+            pltpu.VMEM((H, 2 * KH), BF16),
             dma,
             dma,
             dma,
@@ -869,8 +932,9 @@
         + exchange_scratch()
         + exchange_semaphores()
         + exchange_semaphores()
-        + reduction_scratch(24, HID)
-        + reduction_scratch(48, 128),
+        + reduction_scratch(12)
+        + reduction_scratch(4)
+        + [dma((3,))],
         compiler_params=pltpu.CompilerParams(
             collective_id=0, has_side_effects=True, vmem_limit_bytes=67043328
         ),
@@ -878,12 +942,37 @@
     )(*args)
 
 
+def deliver_kernel(*refs):
+    for source, target in zip(refs[:7], refs[7:]):
+        target[...] = source[...]
+
+
+def deliver(arrays):
+    steps = 8
+    cells = pl.BlockSpec((C // steps, LR, LW), lambda i: (i, 0, 0))
+    grads = pl.BlockSpec((C // steps, HID), lambda i: (i, 0))
+
+    def whole(a):
+        return pl.BlockSpec(a.shape, lambda i: (0,) * a.ndim)
+
+    specs = [cells, cells, grads, grads] + [whole(a) for a in arrays[4:]]
+    return pl.pallas_call(
+        deliver_kernel,
+        grid=(steps,),
+        out_shape=tuple(jax.ShapeDtypeStruct(a.shape, a.dtype) for a in arrays),
+        in_specs=specs,
+        out_specs=specs,
+        name="deliver",
+    )(*arrays)
+
+
 def body(weather, cotangent, spectral_in, spectral_bias, spectral_out, project_in, project_out):
     width, weighted, height = tables()
-    output, grad_weather, grad_pin, grad_pout_t, grad_in, grad_out, grad_bias, _ = layer_call(
+    results = layer_call(
         weather, cotangent, width, weighted, height, spectral_in, spectral_bias, spectral_out,
         project_in, project_out.T,
     )
+    output, grad_weather, grad_pin, grad_pout_t, grad_in, grad_out, grad_bias = deliver(results[:7])
     return output, grad_weather, grad_pin, grad_pout_t.T, grad_in, grad_out, grad_bias
 
 

time: 322 us -> 299 us (0.929); the launches traced: 318 us -> 298 us
  Pallas kernels: 307 us -> 297 us
  local copies, waits for them, and re-layouts: 9.65 us -> 0 us
    pallas_call x1, Pallas kernels: 307 us -> 289 us  [layer_call(): pl.pallas_call(layer_kernel, out_shape=(shape((C, LR, LW), BF16), shape((...]
    unnamed x19 -> x0, local copies, waits for them, and re-layouts: 9.65 us -> none
    pallas_call x0 -> x1, Pallas kernels: none -> 8.49 us  [deliver(): pl.pallas_call(deliver_kernel, grid=(steps,), out_shape=tuple((jax.ShapeD...]
where the time goes in v4:
time: 299 us; the launch traced here: 298 us
  Pallas kernels  297 us (99%)
    pallas_call x1, Pallas kernels, layer_call(): pl.pallas_call(layer_kernel, out_shape=(shape((C, LR, LW), BF16), shape((...  289 us
    pallas_call x1, Pallas kernels, deliver(): pl.pallas_call(deliver_kernel, grid=(steps,), out_shape=tuple((jax.ShapeD...  8.49 us

profile of v4, /device:TPU:1, one launch (start us, length us, event | category | flops | bytes accessed | tf_op | source)
XLA Modules:
  0.0 298.1 jit_solution(16607059351726400969)
XLA Ops:
  0.6 288.8 %layer.1 = (bf16[192,64,128]{2,1,0:T(8,128)(2,1)}, bf16[192,64,128]{2,1,0:T(8,128)(2,1)}, f32[192,768]{1,0:T(8,128)}, f32[192,768]{1,0:T(8,128)}, f32[2,2,96,96]...) custom-call(bf16[192,64,128]{2,1,0:T(8,128)(2,1)} %weather.1, ...), custom_call_target="tpu_custom_call" | custom-call | tf_op jit(solution)/shard_map/layer/pallas_call | solution.py:891
  289.5 8.5 %deliver.1 = (bf16[192,64,128]{2,1,0:T(8,128)(2,1)}, bf16[192,64,128]{2,1,0:T(8,128)(2,1)}, f32[192,768]{1,0:T(8,128)}, f32[192,768]{1,0:T(8,128)}, f32[2,2,96,9...) custom-call(bf16[192,64,128]{2,1,0:T(8,128)(2,1)} %get-tuple-element.21.refs_0_, ...), custom_call_target="tpu_custom_call" | custom-call | tf_op jit(solution)/shard_map/deliver/pallas_call | solution.py:959

commit v5 on v4

--- a/solution.py
+++ b/solution.py
@@ -20,11 +20,13 @@
 
 LR = 64
 LW = 128
-CG = 12
+CG = 6
 CH = 2
 NCH = CG // CH
 NX = 4
-SG = 8
+SG = 4
+FG = 2 * KW // SG
+RW = 4 * LR
 MODES = 2048
 TR = 16
 RB = LR // TR
@@ -42,14 +44,15 @@
     angle = (k[:, None] * np.arange(W)[None, :] % W).astype(np.float32) * np.float32(2.0 * math.pi / W)
     factor = np.float32(1.0 / math.sqrt(W))
     cosine, sine = np.cos(angle) * factor, -np.sin(angle) * factor
-    width = np.stack([cosine.reshape(SG, 32, W), sine.reshape(SG, 32, W)], axis=1).reshape(2 * KW, W)
+    width = np.stack([cosine.reshape(SG, FG // 2, W), sine.reshape(SG, FG // 2, W)], axis=1).reshape(2 * KW, W)
     weight = np.where(k == 0, 1.0, 2.0).astype(np.float32)[:, None]
     weighted = np.stack(
-        [(cosine * weight).reshape(SG, 32, W), (sine * weight).reshape(SG, 32, W)], axis=1
+        [(cosine * weight).reshape(SG, FG // 2, W), (sine * weight).reshape(SG, FG // 2, W)], axis=1
     ).reshape(2 * KW, W)
     m = np.arange(KH)
     frequency = np.where(m < KH // 2, m, m + (H - KH))
-    angle = (np.arange(H)[:, None] * frequency[None, :] % H).astype(np.float32) * np.float32(
+    rows = np.arange(H).reshape(2, SG, 2 * LR).transpose(1, 0, 2).reshape(-1)
+    angle = (rows[:, None] * frequency[None, :] % H).astype(np.float32) * np.float32(
         2.0 * math.pi / H
     )
     factor = np.float32(1.0 / math.sqrt(H))
@@ -85,92 +88,95 @@
         self.s = self.ri // 2
         self.x = self.ci // 2
         self.yh = self.ci % 2
-        self.id1 = self.ci * 2 + self.core
-        self.id2 = self.x * 2 + self.core
+        self.lo = self.s // 4
         self.z = self.s % 4
-        self.id3 = (self.s // 4) * 8 + self.ci
+        self.id1 = (self.ci * 2 + self.lo) * 2 + self.core
+        self.part = self.lo * 2 + self.core
+        self.id2 = self.x * 4 + self.part
+        self.id3 = self.lo * 8 + self.ci
 
     def peer1(self, d):
-        other = (self.id1 + d) % 16
-        return other // 2, other % 2
+        other = (self.id1 + d) % 32
+        return other // 4, other % 4
 
     def peer2(self, e):
-        other = (self.id2 + e) % 8
-        return other // 2, other % 2
+        other = (self.id2 + e) % 16
+        return other // 4, other % 4
 
     def peer3(self, d):
         other = (self.id3 + d) % 16
         return other // 8, other % 8
 
+    def row(self, part, z):
+        return 2 * (4 * (part // 2) + z) + part % 2
+
     def greet(self):
         sem = pltpu.get_barrier_semaphore()
-        for d in range(1, 16):
-            col, core = self.peer1(d)
-            pl.semaphore_signal(sem, inc=1, device_id=(2 * self.s + core, col), device_id_type=MESH)
+        for d in range(1, 32):
+            col, part = self.peer1(d)
+            pl.semaphore_signal(sem, inc=1, device_id=(self.row(part, self.z), col), device_id_type=MESH)
         for e in range(1, SG):
-            s = (self.s + e) % SG
-            pl.semaphore_signal(sem, inc=1, device_id=(2 * s + self.core, self.ci), device_id_type=MESH)
-        other_lo = 1 - self.s // 4
-        for e in range(1, 8):
-            row = 2 * (4 * other_lo + self.z) + self.core
-            pl.semaphore_signal(sem, inc=1, device_id=(row, (self.ci + e) % 8), device_id_type=MESH)
+            z = (self.z + e) % SG
+            pl.semaphore_signal(sem, inc=1, device_id=(self.row(self.part, z), self.ci), device_id_type=MESH)
 
     def barrier(self):
-        pl.semaphore_wait(pltpu.get_barrier_semaphore(), 15 + SG - 1 + 7)
-
-    def first_channel(self, col, core):
-        return (col % 2) * BS + (col // 2) * (2 * CG) + core * CG
+        pl.semaphore_wait(pltpu.get_barrier_semaphore(), 31 + SG - 1)
+
+    def first_channel(self, col, part):
+        return (col % 2) * BS + ((col // 2) * 4 + part) * CG
+
+    def rows_at(self, part, start, count):
+        return pl.ds(pl.multiple_of(part * LR + start, TR), count)
 
     def copy1(self, src, i, d):
-        col, core = self.peer1(d)
-        start = self.first_channel(col, core) + i * CH
-        rows = pl.ds(pl.multiple_of(self.core * LR, LR), LR)
+        col, part = self.peer1(d)
+        start = self.first_channel(col, part) + i * CH
         return pltpu.make_async_remote_copy(
             src_ref=src.at[pl.ds(start, CH)],
-            dst_ref=self.X.at[self.ci, pl.ds(i * CH, CH), rows, :],
+            dst_ref=self.X.at[self.ci, pl.ds(i * CH, CH), self.rows_at(self.part, 0, LR), :],
             send_sem=self.sems[0].at[i, d],
             recv_sem=self.sems[1].at[i, d],
-            device_id=(2 * self.s + core, col),
+            device_id=(self.row(part, self.z), col),
             device_id_type=MESH,
         )
 
     def rows1(self, src, r, d):
-        col, core = self.peer1(d)
-        rows = pl.ds(pl.multiple_of(r * TR, TR), TR)
-        there = pl.ds(pl.multiple_of(self.core * LR + r * TR, TR), TR)
-        return pltpu.make_async_remote_copy(
-            src_ref=src.at[pl.ds(self.first_channel(col, core), CG), rows, :],
-            dst_ref=self.X.at[self.ci, :, there, :],
+        col, part = self.peer1(d)
+        return pltpu.make_async_remote_copy(
+            src_ref=src.at[pl.ds(self.first_channel(col, part), CG), self.rows_at(0, r * TR, TR), :],
+            dst_ref=self.X.at[self.ci, :, self.rows_at(self.part, r * TR, TR), :],
             send_sem=self.sems[0].at[r, d],
             recv_sem=self.sems[1].at[r, d],
-            device_id=(2 * self.s + core, col),
+            device_id=(self.row(part, self.z), col),
             device_id_type=MESH,
         )
 
     def send_rows1(self, src, r):
-        rows = pl.ds(pl.multiple_of(r * TR, TR), TR)
-        there = pl.ds(pl.multiple_of(self.core * LR + r * TR, TR), TR)
-        own = self.first_channel(self.ci, self.core)
-        for d in range(1, 16):
+        own = self.first_channel(self.ci, self.part)
+        for d in range(1, 32):
             self.rows1(src, r, d).start()
-        self.X[self.ci, :, there, :] = src[pl.ds(own, CG), rows, :]
+        self.X[self.ci, :, self.rows_at(self.part, r * TR, TR), :] = src[
+            pl.ds(own, CG), self.rows_at(0, r * TR, TR), :
+        ]
 
     def send1(self, src):
-        rows = pl.ds(pl.multiple_of(self.core * LR, LR), LR)
-        own = self.first_channel(self.ci, self.core)
-        for i in range(NCH):
-            for d in range(1, 16):
+        own = self.first_channel(self.ci, self.part)
+
+        @pl.loop(0, NCH)
+        def _(i):
+            for d in range(1, 32):
                 self.copy1(src, i, d).start()
-        self.X[self.ci, :, rows, :] = src[pl.ds(own, CG)]
+
+        self.X[self.ci, :, self.rows_at(self.part, 0, LR), :] = src[pl.ds(own, CG)]
 
     def copyb(self, i, e):
-        s = (self.s + e) % SG
-        return pltpu.make_async_remote_copy(
-            src_ref=self.O.at[s, pl.ds(i * CH, CH)],
-            dst_ref=self.G.at[self.s, pl.ds(i * CH, CH)],
+        z = (self.z + e) % SG
+        return pltpu.make_async_remote_copy(
+            src_ref=self.O.at[z, pl.ds(i * CH, CH)],
+            dst_ref=self.G.at[self.z, pl.ds(i * CH, CH)],
             send_sem=self.sems[2].at[i, e],
             recv_sem=self.sems[3].at[i, e],
-            device_id=(2 * s + self.core, self.ci),
+            device_id=(self.row(self.part, z), self.ci),
             device_id_type=MESH,
         )
 
@@ -179,35 +185,31 @@
 
             @pl.loop(0, RB)
             def _(r):
-                for d in range(1, 16):
+                for d in range(1, 32):
                     self.rows1(src, r, d).wait_recv()
 
         @pl.loop(0, NCH)
         def _(i):
             if not by_rows:
-                for d in range(1, 16):
+                for d in range(1, 32):
                     self.copy1(src, i, d).wait_recv()
-            for half in range(CH // 2):
-                c = i * CH + 2 * half
-                field = jnp.concatenate(
-                    [self.X[p, pl.ds(c, 2)].reshape(2 * 2 * LR, LW) for p in range(8)], axis=1
-                )
-                spectrum = dot_nt(table[...], field).astype(BF16)
-                for j in range(2):
-                    self.O[:, c + j] = spectrum[:, j * 128 : (j + 1) * 128].reshape(SG, 64, 128)
+            for j in range(CH):
+                c = i * CH + j
+                field = jnp.concatenate([self.X[p, c] for p in range(8)], axis=1)
+                self.O[:, c] = dot_nt(table[...], field).astype(BF16).reshape(SG, FG, RW)
             for e in range(1, SG):
                 self.copyb(i, e).start()
             own = pl.ds(i * CH, CH)
-            self.G[self.s, own] = self.O[self.s, own]
+            self.G[self.z, own] = self.O[self.z, own]
 
     def copyc(self, i, e):
-        x, core = self.peer2(e)
-        return pltpu.make_async_remote_copy(
-            src_ref=self.K.at[x, core, pl.ds(i * CH, CH)],
+        x, part = self.peer2(e)
+        return pltpu.make_async_remote_copy(
+            src_ref=self.K.at[x, part, pl.ds(i * CH, CH)],
             dst_ref=self.Y0.at[self.id2, pl.ds(i * CH, CH)],
             send_sem=self.sems[4].at[i, e],
             recv_sem=self.sems[5].at[i, e],
-            device_id=(2 * self.s + core, 2 * x + self.yh),
+            device_id=(self.row(part, self.z), 2 * x + self.yh),
             device_id_type=MESH,
         )
 
@@ -218,26 +220,26 @@
                 self.copyb(i, e).wait_recv()
             own = pl.ds(i * CH, CH)
             spectrum = jnp.concatenate(
-                [self.G[s, own].reshape(CH * 64, 128) for s in range(SG)], axis=1
+                [self.G[z, own].reshape(CH * FG, RW) for z in range(SG)], axis=1
             )
             for x in range(NX):
                 lanes = slice(x * 128, (x + 1) * 128)
                 shifted = slice(KH + x * 128, KH + (x + 1) * 128)
                 both = jnp.concatenate([table[:, lanes], table[:, shifted]], axis=1)
-                terms = dot_nn(spectrum, both).reshape(CH, 2, 2, 16, 256)
+                terms = dot_nn(spectrum, both).reshape(CH, 2, 4, 16, 256)
                 real = terms[:, 0, :, :, :128] - terms[:, 1, :, :, 128:]
                 imaginary = terms[:, 0, :, :, 128:] + terms[:, 1, :, :, :128]
-                for core in range(2):
-                    self.K[x, core, own, 0] = real[:, core].astype(BF16)
-                    self.K[x, core, own, 1] = imaginary[:, core].astype(BF16)
-            for e in range(1, 8):
+                for part in range(4):
+                    self.K[x, part, own, 0] = real[:, part].astype(BF16)
+                    self.K[x, part, own, 1] = imaginary[:, part].astype(BF16)
+            for e in range(1, 16):
                 self.copyc(i, e).start()
-            self.Y0[self.id2, own] = self.K[self.x, self.core, own]
+            self.Y0[self.id2, own] = self.K[self.x, self.part, own]
 
     def modes(self, out):
         @pl.loop(0, NCH)
         def _(i):
-            for e in range(1, 8):
+            for e in range(1, 16):
                 self.copyc(i, e).wait_recv()
         self.y32[...] = self.Y0[...].astype(F32).reshape(BS * 32, 128)
         for part in range(2):
@@ -247,13 +249,14 @@
                 ].astype(BF16)
 
     def copyz(self, i, e):
-        x, core = self.peer2(e)
-        return pltpu.make_async_remote_copy(
-            src_ref=self.Z0.at[x * 2 + core, pl.ds(i * CH, CH)],
-            dst_ref=self.Q.at[self.x, pl.ds(i * CH, CH), :, pl.ds(pl.multiple_of(self.core * 16, 16), 16), :],
+        x, part = self.peer2(e)
+        columns = pl.ds(pl.multiple_of(self.part * 16, 16), 16)
+        return pltpu.make_async_remote_copy(
+            src_ref=self.Z0.at[x * 4 + part, pl.ds(i * CH, CH)],
+            dst_ref=self.Q.at[self.x, pl.ds(i * CH, CH), :, columns, :],
             send_sem=self.sems[6].at[i, e],
             recv_sem=self.sems[7].at[i, e],
-            device_id=(2 * self.s + core, 2 * x + self.yh),
+            device_id=(self.row(part, self.z), 2 * x + self.yh),
             device_id_type=MESH,
         )
 
@@ -265,142 +268,139 @@
                     self.y32[pl.ds(part * 16 + q * 4 + j, BS, stride=32), :] = block[
                         part * BS : (part + 1) * BS, j * 128 : (j + 1) * 128
                     ]
-        self.Z0[...] = self.y32[...].astype(BF16).reshape(8, CG, 2, 16, 128)
-        for i in range(NCH):
-            for e in range(1, 8):
+        self.Z0[...] = self.y32[...].astype(BF16).reshape(16, CG, 2, 16, 128)
+
+        @pl.loop(0, NCH)
+        def _(i):
+            for e in range(1, 16):
                 self.copyz(i, e).start()
-        self.Q[self.x, :, :, pl.ds(pl.multiple_of(self.core * 16, 16), 16), :] = self.Z0[self.id2]
+
+        columns = pl.ds(pl.multiple_of(self.part * 16, 16), 16)
+        self.Q[self.x, :, :, columns, :] = self.Z0[self.id2]
 
     def copyf(self, i, e):
-        s = (self.s + e) % SG
-        return pltpu.make_async_remote_copy(
-            src_ref=self.BK.at[s, pl.ds(i * CH, CH)],
-            dst_ref=self.F.at[self.s, pl.ds(i * CH, CH)],
+        z = (self.z + e) % SG
+        return pltpu.make_async_remote_copy(
+            src_ref=self.BK.at[z, pl.ds(i * CH, CH)],
+            dst_ref=self.F.at[self.z, pl.ds(i * CH, CH)],
             send_sem=self.sems[8].at[i, e],
             recv_sem=self.sems[9].at[i, e],
-            device_id=(2 * s + self.core, self.ci),
+            device_id=(self.row(self.part, z), self.ci),
             device_id_type=MESH,
         )
 
     def height_inverse(self, table):
         @pl.loop(0, NCH)
         def _(i):
-            for e in range(1, 8):
+            for e in range(1, 16):
                 self.copyz(i, e).wait_recv()
             own = pl.ds(i * CH, CH)
-            modes = jnp.concatenate([self.Q[x, own].reshape(CH * 64, 128) for x in range(NX)], axis=1)
-            for q in range(4):
-                rows = slice(q * 256, (q + 1) * 256)
-                first = dot_nt(modes, table[rows, :KH]).reshape(CH, 2, 32, 256)
-                second = dot_nt(modes, table[rows, KH:]).reshape(CH, 2, 32, 256)
-                real = (first[:, 0] + second[:, 1]).astype(BF16)
-                imaginary = (first[:, 1] - second[:, 0]).astype(BF16)
-                for j in range(2):
-                    lanes = slice(j * 128, (j + 1) * 128)
-                    self.BK[2 * q + j, own, :32, :] = real[:, :, lanes]
-                    self.BK[2 * q + j, own, 32:, :] = imaginary[:, :, lanes]
+            modes = jnp.concatenate([self.Q[x, own].reshape(CH * FG, 128) for x in range(NX)], axis=1)
+            for z in range(SG):
+                rows = slice(z * RW, (z + 1) * RW)
+                first = dot_nt(modes, table[rows, :KH]).reshape(CH, 2, FG // 2, RW)
+                second = dot_nt(modes, table[rows, KH:]).reshape(CH, 2, FG // 2, RW)
+                self.BK[z, own, : FG // 2, :] = (first[:, 0] + second[:, 1]).astype(BF16)
+                self.BK[z, own, FG // 2 :, :] = (first[:, 1] - second[:, 0]).astype(BF16)
             for e in range(1, SG):
                 self.copyf(i, e).start()
-            self.F[self.s, own] = self.BK[self.s, own]
+            self.F[self.z, own] = self.BK[self.z, own]
 
     def copyo(self, out, i, d):
-        col, core = self.peer1(d)
-        start = self.first_channel(self.ci, self.core) + i * CH
-        rows = pl.ds(pl.multiple_of(core * LR, LR), LR)
-        return pltpu.make_async_remote_copy(
-            src_ref=self.FO.at[col, pl.ds(i * CH, CH), rows, :],
+        col, part = self.peer1(d)
+        start = self.first_channel(self.ci, self.part) + i * CH
+        return pltpu.make_async_remote_copy(
+            src_ref=self.FO.at[col, pl.ds(i * CH, CH), self.rows_at(part, 0, LR), :],
             dst_ref=out.at[pl.ds(start, CH)],
             send_sem=self.sems[10].at[i, d],
             recv_sem=self.sems[11].at[i, d],
-            device_id=(2 * self.s + core, col),
+            device_id=(self.row(part, self.z), col),
             device_id_type=MESH,
         )
 
     def rowso(self, out, r, d):
-        col, core = self.peer1(d)
-        rows = pl.ds(pl.multiple_of(core * LR + r * TR, TR), TR)
-        there = pl.ds(pl.multiple_of(r * TR, TR), TR)
-        return pltpu.make_async_remote_copy(
-            src_ref=self.FO.at[col, :, rows, :],
-            dst_ref=out.at[pl.ds(self.first_channel(self.ci, self.core), CG), there, :],
+        col, part = self.peer1(d)
+        start = self.first_channel(self.ci, self.part)
+        return pltpu.make_async_remote_copy(
+            src_ref=self.FO.at[col, :, self.rows_at(part, r * TR, TR), :],
+            dst_ref=out.at[pl.ds(start, CG), self.rows_at(0, r * TR, TR), :],
             send_sem=self.sems[10].at[r, d],
             recv_sem=self.sems[11].at[r, d],
-            device_id=(2 * self.s + core, col),
+            device_id=(self.row(part, self.z), col),
             device_id_type=MESH,
         )
 
     def width_inverse(self, out, table, by_rows):
-        rows = pl.ds(pl.multiple_of(self.core * LR, LR), LR)
-        start = self.first_channel(self.ci, self.core)
+        start = self.first_channel(self.ci, self.part)
 
         @pl.loop(0, NCH)
         def _(i):
             for e in range(1, SG):
                 self.copyf(i, e).wait_recv()
-            for half in range(CH // 2):
-                c = i * CH + 2 * half
-                spectrum = jnp.concatenate(
-                    [self.F[:, c].reshape(2 * KW, 128), self.F[:, c + 1].reshape(2 * KW, 128)], axis=1
-                )
-                turned = spectrum.T
+            for j in range(CH):
+                c = i * CH + j
+                turned = self.F[:, c].reshape(2 * KW, RW).T
                 for q in range(4):
                     field = dot_nn(turned, table[:, q * 256 : (q + 1) * 256]).astype(BF16)
-                    for j in range(2):
-                        self.FO[2 * q + j, pl.ds(c, 2)] = field[:, j * 128 : (j + 1) * 128].reshape(
-                            2, 128, 128
-                        )
+                    for half in range(2):
+                        self.FO[2 * q + half, c] = field[:, half * 128 : (half + 1) * 128]
             if not by_rows:
-                for d in range(1, 16):
+                for d in range(1, 32):
                     self.copyo(out, i, d).start()
-            out[pl.ds(start + i * CH, CH)] = self.FO[self.ci, pl.ds(i * CH, CH), rows, :]
+            out[pl.ds(start + i * CH, CH)] = self.FO[
+                self.ci, pl.ds(i * CH, CH), self.rows_at(self.part, 0, LR), :
+            ]
 
         if by_rows:
 
             @pl.loop(0, RB)
             def _(r):
-                for d in range(1, 16):
+                for d in range(1, 32):
                     self.rowso(out, r, d).start()
 
     def drain(self, src, first):
         @pl.loop(0, RB if first else NCH)
         def _(i):
-            for d in range(1, 16):
+            for d in range(1, 32):
                 (self.rows1 if first else self.copy1)(src, i, d).wait_send()
 
         @pl.loop(0, NCH)
         def _(i):
-            for e in range(1, 8):
+            for e in range(1, SG):
                 self.copyb(i, e).wait_send()
+                self.copyf(i, e).wait_send()
+            for e in range(1, 16):
                 self.copyc(i, e).wait_send()
                 self.copyz(i, e).wait_send()
-                self.copyf(i, e).wait_send()
 
     def drain_out(self, out, by_rows):
         @pl.loop(0, RB if by_rows else NCH)
         def _(i):
-            for d in range(1, 16):
+            for d in range(1, 32):
                 (self.rowso if by_rows else self.copyo)(out, i, d).wait_send()
 
 
 def exchange_scratch():
+    cells = pltpu.VMEM((8, CG, RW, LW), BF16)
+    columns = pltpu.VMEM((SG, CG, FG, RW), BF16)
     return [
-        pltpu.VMEM((8, CG, 2 * LR, LW), BF16),
-        pltpu.VMEM((SG, CG, 64, 128), BF16),
-        pltpu.VMEM((SG, CG, 64, 128), BF16),
-        pltpu.VMEM((NX, 2, CG, 2, 16, 128), BF16),
-        pltpu.VMEM((8, CG, 2, 16, 128), BF16),
+        cells,
+        columns,
+        columns,
+        pltpu.VMEM((NX, 4, CG, 2, 16, 128), BF16),
+        pltpu.VMEM((16, CG, 2, 16, 128), BF16),
         pltpu.VMEM((BS * 32, 128), F32),
-        pltpu.VMEM((8, CG, 2, 16, 128), BF16),
-        pltpu.VMEM((NX, CG, 2, 32, 128), BF16),
-        pltpu.VMEM((SG, CG, 64, 128), BF16),
-        pltpu.VMEM((SG, CG, 64, 128), BF16),
-        pltpu.VMEM((8, CG, 2 * LR, LW), BF16),
+        pltpu.VMEM((16, CG, 2, 16, 128), BF16),
+        pltpu.VMEM((NX, CG, 2, 64, 128), BF16),
+        columns,
+        columns,
+        cells,
     ]
 
 
 def exchange_semaphores():
     most = max(NCH, RB)
-    pairs = [(most, 16), (NCH, 8), (NCH, 8), (NCH, 8), (NCH, 8), (most, 16)]
+    pairs = [(most, 32), (NCH, SG), (NCH, 16), (NCH, 16), (NCH, SG), (most, 32)]
     return [pltpu.SemaphoreType.DMA(shape) for shape in pairs for _ in range(2)]
 
 
@@ -787,7 +787,7 @@
 
     @pl.loop(0, RB)
     def _(r):
-        for d in range(1, 16):
+        for d in range(1, 32):
             ex.rowso(filtered, r, d).wait_recv()
         next_cot(r).wait()
         token_rows(
@@ -834,7 +834,7 @@
 
     @pl.loop(0, NCH)
     def _(i):
-        for d in range(1, 16):
+        for d in range(1, 32):
             back.copyo(filtered, i, d).wait_recv()
 
     @pl.loop(0, RB)

time: 299 us -> 300 us (level)
  no operation moved by 1% of the time
where the time goes in v5:
time: 300 us
  Pallas kernels  299 us (100%)
    pallas_call x1, Pallas kernels, layer_call(): pl.pallas_call(layer_kernel, out_shape=(shape((C, LR, LW), BF16), shape((...  290 us
    pallas_call x1, Pallas kernels, deliver(): pl.pallas_call(deliver_kernel, grid=(steps,), out_shape=tuple((jax.ShapeD...  8.49 us

profile of v5, /device:TPU:1, one launch (start us, length us, event | category | flops | bytes accessed | tf_op | source)
XLA Modules:
  0.0 299.7 jit_solution(2046288567131607669)
XLA Ops:
  0.6 290.4 %layer.1 = (bf16[192,64,128]{2,1,0:T(8,128)(2,1)}, bf16[192,64,128]{2,1,0:T(8,128)(2,1)}, f32[192,768]{1,0:T(8,128)}, f32[192,768]{1,0:T(8,128)}, f32[2,2,96,96]...) custom-call(bf16[192,64,128]{2,1,0:T(8,128)(2,1)} %weather.1, ...), custom_call_target="tpu_custom_call" | custom-call | tf_op jit(solution)/shard_map/layer/pallas_call | solution.py:891
  291.1 8.5 %deliver.1 = (bf16[192,64,128]{2,1,0:T(8,128)(2,1)}, bf16[192,64,128]{2,1,0:T(8,128)(2,1)}, f32[192,768]{1,0:T(8,128)}, f32[192,768]{1,0:T(8,128)}, f32[2,2,96,9...) custom-call(bf16[192,64,128]{2,1,0:T(8,128)(2,1)} %get-tuple-element.21.refs_0_, ...), custom_call_target="tpu_custom_call" | custom-call | tf_op jit(solution)/shard_map/deliver/pallas_call | solution.py:959
